TPU v7x, 128 devices: a whole 4x4x4 slice. The times are simulated.
128 devices in a mesh: lat: 8 (over x, core), lon: 16 (over z, y).
Axes of the slice: x: 4, y: 4, z: 4, core: 2. Of those that a mesh axis runs over, the one named last changes fastest.
Arguments:
- latent_field: float32 [32, 8, 128, 2048], P(None, None, 'lat', 'lon'), may hold values from -6 to 6
- east_courant: float32 [8, 128, 2048], P(None, 'lat', 'lon'), may hold values from -0.45 to 0.45
- north_courant: float32 [8, 128, 2048], P(None, 'lat', 'lon'), may hold values from -0.45 to 0.45
- mixing: float32 [7, 128, 2048], P(None, 'lat', 'lon'), may hold values from 0.2 to 5
- sunlit: int32 [8, 128], P('lat', 'lon'), may hold values from 0 to 1, as said below
- decode_w: bfloat16 [224, 32], replicated, may hold values from -1 to 1
- react_a: bfloat16 [256, 224], replicated, may hold values from -0.375 to 0.375
- react_b: bfloat16 [256, 224], replicated, may hold values from -0.375 to 0.375
- stoich: bfloat16 [224, 256], replicated, may hold values from -0.375 to 0.375
- encode_w: bfloat16 [32, 224], replicated, may hold values from -0.375 to 0.375
- rate_const: float32 [256], replicated, may hold values from 0.05 to 0.5
Outputs:
- advanced: float32 [32, 8, 128, 2048], P(None, None, 'lat', 'lon')
Inputs may be any that keep to these rules, and one draw needn't show every extreme that they name: In each row of blocks the sunlit blocks form one run, periodic in longitude, of 32 to 96 blocks.
All inputs are finite; a program needn't handle non-finite values.
Results may differ from a plain program's by a relative error of at most 0.0035.
Values may be sent and summed in bfloat16 or wider, within the bound.
A program may use at most 128 MiB of HBM per device.

v0:
```python
import jax
import jax.numpy as jnp
from jax import lax
from jax.sharding import PartitionSpec as P

BLOCK = 16
SUBSTEPS = 2
STEPS = 2


def padded_2(array, sides, width):
    for axis, dim in sides:
        size, length = (lax.axis_size(axis), array.shape[dim])
        up = [(i, (i + 1) % size) for i in range(size)]
        down = [(j, i) for i, j in up]
        last = lax.slice_in_dim(array, length - width, length, axis=dim)
        initial = lax.slice_in_dim(array, 0, width, axis=dim)
        before = lax.ppermute(last, axis, up)
        after = lax.ppermute(initial, axis, down)
        array = jnp.concatenate([before, array, after], axis=dim)
    return array


def advect(tracers, east_courant, north_courant, north_open):
    n_species = tracers.shape[0]
    stacked = jnp.concatenate([tracers, east_courant[None], north_courant[None]], 0)
    padded = padded_2(stacked, (("lat", 2), ("lon", 3)), 1)
    values = padded[:n_species]
    east_speed = padded[n_species : n_species + 1]
    north_speed = padded[n_species + 1 : n_species + 2]
    inner = values[:, :, 1:-1, 1:-1]
    east_face = (
        jnp.maximum(east_speed[:, :, 1:-1, :-1], 0.0) * values[:, :, 1:-1, :-1]
        + jnp.minimum(east_speed[:, :, 1:-1, 1:], 0.0) * values[:, :, 1:-1, 1:]
    )
    north_face = (
        jnp.maximum(north_speed[:, :, :-1, 1:-1], 0.0) * values[:, :, :-1, 1:-1]
        + jnp.minimum(north_speed[:, :, 1:, 1:-1], 0.0) * values[:, :, 1:, 1:-1]
    )
    north_face = jnp.where(north_open[:, None], north_face, 0.0)
    return (
        inner
        - (east_face[:, :, :, 1:] - east_face[:, :, :, :-1])
        - (north_face[:, :, 1:] - north_face[:, :, :-1])
    )


def diffuse(tracers, mixing):
    n_levels = tracers.shape[1]
    sweep_upper = []
    sweep_right = []
    for level_index in range(n_levels):
        below_mix = mixing[level_index - 1][None] if level_index > 0 else 0.0
        above_mix = mixing[level_index][None] if level_index < n_levels - 1 else 0.0
        diagonal = 1.0 + below_mix + above_mix
        if level_index > 0:
            pivot_value = diagonal + below_mix * sweep_upper[-1]
            right_side = tracers[:, level_index] + below_mix * sweep_right[-1]
        else:
            pivot_value = diagonal
            right_side = tracers[:, 0]
        sweep_upper.append(-above_mix / pivot_value)
        sweep_right.append(right_side / pivot_value)
    solved = [sweep_right[-1]]
    for level_index in range(n_levels - 2, -1, -1):
        solved.insert(0, sweep_right[level_index] - sweep_upper[level_index] * solved[0])
    return jnp.stack(solved, 1)


def react_all(latent_in, weights):
    decode_w, react_a, react_b, stoich, encode_w, rate_const = weights
    current = latent_in.astype(jnp.float32)
    summed = jnp.zeros(current.shape, jnp.float32)
    species = jnp.einsum(
        "ps,bsc->bpc", decode_w, latent_in, preferred_element_type=jnp.float32
    ).astype(jnp.bfloat16)
    for substep in range(SUBSTEPS):
        if substep > 0:
            species = jnp.einsum(
                "ps,bsc->bpc",
                decode_w,
                current.astype(jnp.bfloat16),
                preferred_element_type=jnp.float32,
            ).astype(jnp.bfloat16)
        react_first = jnp.einsum(
            "rp,bpc->brc", react_a, species, preferred_element_type=jnp.float32
        )
        react_second = jnp.einsum(
            "rp,bpc->brc", react_b, species, preferred_element_type=jnp.float32
        )
        rate_values = (rate_const[None, :, None] * react_first * react_second).astype(jnp.bfloat16)
        tendency = jnp.einsum(
            "pr,brc->bpc", stoich, rate_values, preferred_element_type=jnp.float32
        ).astype(jnp.bfloat16)
        increment = jnp.einsum(
            "sp,bpc->bsc", encode_w, tendency, preferred_element_type=jnp.float32
        ).astype(jnp.bfloat16)
        increment = lax.optimization_barrier(increment).astype(jnp.float32)
        summed = summed + increment
        current = current + increment
    return summed.astype(jnp.bfloat16)


def on_device(
    latent_field,
    east_courant,
    north_courant,
    mixing,
    sunlit,
    decode_w,
    react_a,
    react_b,
    stoich,
    encode_w,
    rate_const,
):
    n_species, n_levels, tile_rows, tile_cols = latent_field.shape
    n_blocks = tile_cols // BLOCK
    lon_devices = lax.axis_size("lon")
    lat_devices = lax.axis_size("lat")
    lon_index = lax.axis_index("lon")
    grid_rows = tile_rows * lat_devices
    face_rows = jnp.arange(tile_rows + 1) + lax.axis_index("lat") * tile_rows
    north_open = face_rows % grid_rows != 0
    sun_mask = sunlit[0]
    column_sun = jnp.repeat(sun_mask, BLOCK)
    weights = (decode_w, react_a, react_b, stoich, encode_w, rate_const)
    block_cells = n_levels * tile_rows * BLOCK
    capacity = -(-n_blocks // lon_devices)
    n_slots = lon_devices * capacity
    busy_slots = (3 * n_blocks + 3) // 4
    my_count = jnp.sum(sun_mask).reshape(1)
    all_counts = lax.all_gather(my_count, "lon", axis=0, tiled=True)
    all_offsets = jnp.cumsum(all_counts) - all_counts
    my_offset = all_offsets[lon_index]
    slot_ids = jnp.arange(n_slots)
    slot_turn = slot_ids % capacity
    slot_owner = slot_ids // capacity
    wanted = (slot_owner - my_offset) % lon_devices + slot_turn * lon_devices
    sun_rank = jnp.cumsum(sun_mask) - sun_mask
    table = ((sun_mask[None, :] > 0) & (sun_rank[None, :] == wanted[:, None])).astype(jnp.int32)
    chosen = jnp.sum(table * jnp.arange(n_blocks)[None, :], axis=1)
    home_slot = jnp.sum(table * slot_ids[:, None], axis=0)
    arriving = (lon_index - all_offsets)[:, None] % lon_devices + jnp.arange(capacity)[
        None, :
    ] * lon_devices
    arriving_live = (arriving < all_counts[:, None]).astype(jnp.int32).reshape(-1)
    live_order = jnp.argsort(1 - arriving_live, stable=True)[:busy_slots]
    for step_index in range(STEPS):
        tracers = diffuse(advect(latent_field, east_courant, north_courant, north_open), mixing)
        latent_blocks = (
            tracers.astype(jnp.bfloat16)
            .reshape(n_species, n_levels, tile_rows, n_blocks, BLOCK)
            .transpose(3, 0, 1, 2, 4)
            .reshape(n_blocks, n_species, block_cells)
        )
        outgoing = jnp.take(latent_blocks, chosen, axis=0).reshape(
            lon_devices, capacity, n_species, block_cells
        )
        received = lax.all_to_all(outgoing, "lon", split_axis=0, concat_axis=0, tiled=True)
        arrived = received.reshape(n_slots, n_species, block_cells)
        reacted = react_all(jnp.take(arrived, live_order, axis=0), weights)
        increments = (
            jnp.zeros((n_slots, n_species, block_cells), jnp.bfloat16).at[live_order].set(reacted)
        )
        returned = lax.all_to_all(
            increments.reshape(lon_devices, capacity, n_species, block_cells),
            "lon",
            split_axis=0,
            concat_axis=0,
            tiled=True,
        )
        per_block = jnp.take(returned.reshape(n_slots, n_species, block_cells), home_slot, axis=0)
        tile_increment = (
            per_block.reshape(n_blocks, n_species, n_levels, tile_rows, BLOCK)
            .transpose(1, 2, 3, 0, 4)
            .reshape(n_species, n_levels, tile_rows, tile_cols)
        )
        latent_field = tracers + jnp.where(
            column_sun[None, None, None, :] > 0, tile_increment.astype(jnp.float32), 0.0
        )
    return latent_field


def solution(mesh):
    placed = (
        P(None, None, "lat", "lon"),
        P(None, "lat", "lon"),
        P(None, "lat", "lon"),
        P(None, "lat", "lon"),
        P("lat", "lon"),
        P(),
        P(),
        P(),
        P(),
        P(),
        P(),
    )
    return jax.shard_map(
        on_device,
        mesh=mesh,
        in_specs=placed,
        out_specs=P(None, None, "lat", "lon"),
        check_vma=False,
    )
```

profile of v0, /device:TPU:6, one launch (start us, length us, event | category | flops | bytes accessed | tf_op | source)
XLA Modules:
  0.0 467.5 jit_solution(17237713308163843223)
XLA Ops:
  7.2 17.7 %all-reduce = s32[16]{0:T(128)S(1)} all-reduce(s32[16]{0:T(128)S(1)} %dynamic-update-slice), channel_id=1, replica_groups=mesh['lat'=8,'lon'=16] {'lon'}, use_global_device_ids=true, to_apply=%add | all-reduce | flops 16 | bytes 128
  27.9 3.1 fusion.201
  30.9 2.9 copy.255
  34.5 2.9 copy.259
  37.4 4.7 %collective-permute-start.3 = (f32[34,8,18,1]{0,1,3,2:T(8,128)S(1)}, f32[34,8,18,1]{0,1,3,2:T(8,128)S(1)}, u32[]{:S(2)}, u32[]{:S(2)}) collective-permute-start(f32[34,8,18,1]{0,1,3,2:T(8,128)S(1)} %copy.259), channel_id=1, source_target_pairs={{1,0},{2,1},{3,2},{4,3},{5,4},{6,5},{7,6},{8,7},{9,8},{10,9},{11,1... | collective-permute-start | bytes 58760 | tf_op jit(solution)/shard_map/ppermute | solution.py:19
  51.6 3.5 fusion.64
  56.8 3.3 fusion.185
  81.1 5.4 %copy.273 = bf16[8,32,8,16,16]{1,4,3,2,0:T(8,128)(2,1)} copy(bf16[8,32,8,16,16]{1,4,0,3,2:T(8,128)(2,1)} %bitcast.249) | data formatting | bytes 2097152 | tf_op jit(solution)/shard_map/transpose | solution.py:154
  86.6 3.5 copy.274
  92.3 4.8 %all-to-all-start = ((bf16[16,1,32,2048]{3,2,1,0:T(8,128)(2,1)}), bf16[16,1,32,2048]{3,2,1,0:T(8,128)(2,1)S(1)}, u32[]{:S(2)}, u32[]{:S(2)}) async-start(bf16[16,1,32,2048]{3,2,1,0:T(8,128)(2,1)} %select_bitcast_fusion.1), calls=%async_computation | async-start | bytes 4194304 | tf_op jit(solution)/shard_map/all_to_all | solution.py:160
  98.5 23.6 %all-to-all-done = bf16[16,1,32,2048]{3,2,1,0:T(8,128)(2,1)S(1)} async-done(((bf16[16,1,32,2048]{3,2,1,0:T(8,128)(2,1)}), bf16[16,1,32,2048]{3,2,1,0:T(8,128)(2,1)S(1)}, u32[]{:S(2)}, u32[]{:S(2)}) %all-to-all-start) | async-done | bytes 2097184 | tf_op jit(solution)/shard_map/all_to_all | solution.py:160
  126.9 6.5 %fusion.36 = f32[6,2048,256]{2,1,0:T(8,128)} fusion(bf16[6,2048,224]{1,2,0:T(8,128)(2,1)S(1)} %convolution_convert_fusion.3, bf16[256,224]{0,1:T(8,128)(2,1)S(1)} %copy-done), kind=kOutput, calls=%fused_computation.44 | convolution fusion | flops 1409286144 | bytes 18202624 | tf_op jit(solution)/shard_map/rp,bpc->brc/dot_general | solution.py:88
  133.4 14.9 %fusion.1 = bf16[6,2048,224]{1,2,0:T(8,128)(2,1)} fusion(f32[6,2048,256]{2,1,0:T(8,128)} %fusion.36, f32[256]{0:T(256)S(1)} %copy-done.88, bf16[6,2048,224]{1,2,0:T(8,128)(2,1)} %copy-done.3, bf16[224,256]{1,0:T(8,128)(2,1)S(1)} %copy-done.35, bf16[256,224]{0,1:T(8,128)(2,1)S(1)} %copy-done.37), kind=kOutput, calls=%fused_computation.13 | convolution fusion | flops 2828009472 | bytes 23823360 | tf_op jit(solution)/shard_map/pr,brc->bpc/dot_general | solution.py:92
  148.3 3.6 fusion.87
  156.2 6.5 %fusion.30 = f32[6,2048,256]{2,1,0:T(8,128)} fusion(bf16[6,2048,224]{1,2,0:T(8,128)(2,1)S(1)} %convolution_convert_fusion.2, bf16[256,224]{0,1:T(8,128)(2,1)S(1)} %copy-done), kind=kOutput, calls=%fused_computation.38 | convolution fusion | flops 1409286144 | bytes 18202624 | tf_op jit(solution)/shard_map/rp,bpc->brc/dot_general | solution.py:88
  162.7 14.9 %fusion.4 = bf16[6,2048,224]{1,2,0:T(8,128)(2,1)} fusion(f32[6,2048,256]{2,1,0:T(8,128)} %fusion.30, f32[256]{0:T(256)S(1)} %copy-done.88, bf16[6,2048,224]{1,2,0:T(8,128)(2,1)} %copy-done.2, bf16[224,256]{1,0:T(8,128)(2,1)S(1)} %copy-done.35, bf16[256,224]{0,1:T(8,128)(2,1)S(1)} %copy-done.37), kind=kOutput, calls=%fused_computation.15 | convolution fusion | flops 2828009472 | bytes 23823360 | tf_op jit(solution)/shard_map/pr,brc->bpc/dot_general | solution.py:92
  177.6 3.6 fusion.84
  183.0 2.8 scatter_fusion
  185.9 4.3 all-to-all-start.1
  190.5 6.3 %stack.58 = f32[32,8,16,128]{3,1,2,0:T(8,128)} concatenate(f32[32,1,16,128]{3,1,2,0:T(1,128)} %get-tuple-element.59, f32[32,1,16,128]{3,1,2,0:T(1,128)} %copy-done.22, f32[32,1,16,128]{3,1,2,0:T(1,128)} %copy-done.21, f32[32,1,16,128]{3,1,2,0:T(1,128)} %copy-done.20, f32[32,1,16,128]{3,1,2,0:T(1,128)S(1)} %copy-done.19, f32[32,1,16,128]{3,1,2,0:T(1,128)S(1)} %copy-done.17, ...), dimensions={1} | concatenate | bytes 4194304 | tf_op jit(solution)/shard_map/stack | solution.py:67
  196.8 18.4 %all-to-all-done.1 = bf16[16,1,32,2048]{3,2,1,0:T(8,128)(2,1)S(1)} async-done(((bf16[16,1,32,2048]{3,2,1,0:T(8,128)(2,1)}), bf16[16,1,32,2048]{3,2,1,0:T(8,128)(2,1)S(1)}, u32[]{:S(2)}, u32[]{:S(2)}) %all-to-all-start.1) | async-done | bytes 2097184 | tf_op jit(solution)/shard_map/all_to_all | solution.py:166
  216.1 4.8 %copy.279 = f32[8,32,2048]{1,2,0:T(8,128)} copy(f32[8,32,2048]{2,1,0:T(8,128)S(1)} %select_convert_fusion.1) | data formatting | bytes 4194304 | tf_op jit(solution)/shard_map/convert_element_type | solution.py:180
  220.8 8.0 %copy.280 = f32[32,8,16,8,16]{0,4,3,2,1:T(8,128)} copy(f32[32,8,16,8,16]{0,4,2,1,3:T(8,128)} %bitcast.243) | data formatting | bytes 4194304 | tf_op jit(solution)/shard_map/convert_element_type | solution.py:180
  228.9 6.5 %copy.281 = f32[32,8,16,128]{3,1,2,0:T(8,128)} copy(f32[32,8,16,128]{0,3,2,1:T(8,128)} %bitcast.244) | data formatting | bytes 4194304 | tf_op jit(solution)/shard_map/convert_element_type | solution.py:180
  239.7 2.7 collective-permute-done.4
  242.6 3.1 fusion.200
  245.7 2.9 copy.284
  249.7 2.9 copy.288
  252.5 4.3 collective-permute-start.7
  258.6 2.6 copy.285
  266.4 5.4 %fusion.61 = f32[32,8,16,129]{3,1,2,0:T(8,128)S(1)} fusion(f32[34,8,18,1]{3,1,2,0:T(8,128)S(1)} %copy-done.7, f32[34,8,1,128]{3,1,2,0:T(8,128)S(1)} %collective-permute-done.5, f32[34,8,1,128]{3,1,2,0:T(8,128)S(1)} %collective-permute-done.4, f32[1,8,16,128]{3,1,2,0:T(8,128)S(1)} %get-tuple-element.91, f32[1,8,16,128]{3,1,2,0:T(8,128)S(1)} %get-tuple-element.93, ...), kind=kLoop, calls=%fused_computation.58 | loop fusion | flops 6868992 | bytes 4791552 | tf_op jit(solution)/shard_map/add | solution.py:33
  273.0 3.3 fusion.170
  296.5 5.4 %copy.300 = bf16[8,32,8,16,16]{1,4,3,2,0:T(8,128)(2,1)} copy(bf16[8,32,8,16,16]{1,4,0,3,2:T(8,128)(2,1)} %bitcast.250) | data formatting | bytes 2097152 | tf_op jit(solution)/shard_map/transpose | solution.py:154
  302.0 3.5 copy.301
  307.2 35.1 %all_to_all.20 = bf16[16,1,32,2048]{3,2,1,0:T(8,128)(2,1)S(1)} all-to-all(bf16[16,1,32,2048]{3,2,1,0:T(8,128)(2,1)S(1)} %select_bitcast_fusion), channel_id=1, replica_groups=mesh['lat'=8,'lon'=16] {'lon'}, dimensions={0} | all-to-all | bytes 4194304 | tf_op jit(solution)/shard_map/all_to_all | solution.py:160
  347.2 6.5 %fusion.24 = f32[6,2048,256]{2,1,0:T(8,128)} fusion(bf16[6,2048,224]{1,2,0:T(8,128)(2,1)S(1)} %convolution_convert_fusion.1, bf16[256,224]{0,1:T(8,128)(2,1)S(1)} %copy-done), kind=kOutput, calls=%fused_computation.32 | convolution fusion | flops 1409286144 | bytes 18202624 | tf_op jit(solution)/shard_map/rp,bpc->brc/dot_general | solution.py:88
  353.7 14.9 %fusion.7 = bf16[6,2048,224]{1,2,0:T(8,128)(2,1)} fusion(f32[6,2048,256]{2,1,0:T(8,128)} %fusion.24, f32[256]{0:T(256)S(1)} %copy-done.89, bf16[6,2048,224]{1,2,0:T(8,128)(2,1)} %copy-done.4, bf16[224,256]{1,0:T(8,128)(2,1)S(1)} %copy-done.36, bf16[256,224]{0,1:T(8,128)(2,1)S(1)} %copy-done.38), kind=kOutput, calls=%fused_computation.17 | convolution fusion | flops 2828009472 | bytes 23823360 | tf_op jit(solution)/shard_map/pr,brc->bpc/dot_general | solution.py:92
  368.5 3.6 fusion.81
  376.5 6.5 %fusion.18 = f32[6,2048,256]{2,1,0:T(8,128)} fusion(bf16[6,2048,224]{1,2,0:T(8,128)(2,1)S(1)} %convolution_convert_fusion, bf16[256,224]{0,1:T(8,128)(2,1)S(1)} %copy-done), kind=kOutput, calls=%fused_computation.26 | convolution fusion | flops 1409286144 | bytes 18202624 | tf_op jit(solution)/shard_map/rp,bpc->brc/dot_general | solution.py:88
  383.0 14.9 %fusion.10 = bf16[6,2048,224]{1,2,0:T(8,128)(2,1)} fusion(f32[6,2048,256]{2,1,0:T(8,128)} %fusion.18, f32[256]{0:T(256)S(1)} %copy-done.89, bf16[6,2048,224]{1,2,0:T(8,128)(2,1)} %copy-done.1, bf16[224,256]{1,0:T(8,128)(2,1)S(1)} %copy-done.36, bf16[256,224]{0,1:T(8,128)(2,1)S(1)} %copy-done.38), kind=kOutput, calls=%fused_computation.19 | convolution fusion | flops 2828009472 | bytes 23823360 | tf_op jit(solution)/shard_map/pr,brc->bpc/dot_general | solution.py:92
  397.8 3.6 fusion.78
  403.3 2.8 scatter_fusion.1
  406.1 4.2 all-to-all-start.3
  410.4 6.2 %stack.68 = f32[32,8,16,128]{3,1,2,0:T(8,128)} concatenate(f32[32,1,16,128]{3,1,2,0:T(1,128)} %get-tuple-element.34, f32[32,1,16,128]{3,1,2,0:T(1,128)} %copy-done.32, f32[32,1,16,128]{3,1,2,0:T(1,128)} %copy-done.31, f32[32,1,16,128]{3,1,2,0:T(1,128)S(1)} %copy-done.30, f32[32,1,16,128]{3,1,2,0:T(1,128)S(1)} %copy-done.28, f32[32,1,16,128]{3,1,2,0:T(1,128)S(1)} %copy-done.26, ...), dimensions={1} | concatenate | bytes 4194304 | tf_op jit(solution)/shard_map/stack | solution.py:67
  416.6 27.5 %all-to-all-done.3 = bf16[16,1,32,2048]{3,2,1,0:T(8,128)(2,1)S(1)} async-done(((bf16[16,1,32,2048]{3,2,1,0:T(8,128)(2,1)}), bf16[16,1,32,2048]{3,2,1,0:T(8,128)(2,1)S(1)}, u32[]{:S(2)}, u32[]{:S(2)}) %all-to-all-start.3) | async-done | bytes 2097184 | tf_op jit(solution)/shard_map/all_to_all | solution.py:166
  445.1 4.7 %copy.306 = f32[8,32,2048]{1,2,0:T(8,128)} copy(f32[8,32,2048]{2,1,0:T(8,128)S(1)} %select_convert_fusion) | data formatting | bytes 4194304 | tf_op jit(solution)/shard_map/convert_element_type | solution.py:180
  449.8 8.0 %copy.307 = f32[32,8,16,8,16]{0,4,3,2,1:T(8,128)} copy(f32[32,8,16,8,16]{0,4,2,1,3:T(8,128)} %bitcast.245) | data formatting | bytes 4194304 | tf_op jit(solution)/shard_map/convert_element_type | solution.py:180
  457.8 5.5 %copy.308 = f32[32,8,16,128]{3,1,2,0:T(8,128)S(1)} copy(f32[32,8,16,128]{0,3,2,1:T(8,128)} %bitcast.246) | data formatting | bytes 4194304 | tf_op jit(solution)/shard_map/convert_element_type | solution.py:180
  (349 shorter events, 108.7 us)
Async XLA Ops:
  0.0 126.9 %copy-start = (bf16[256,224]{0,1:T(8,128)(2,1)S(1)}, bf16[256,224]{0,1:T(8,128)(2,1)}, u32[]{:S(2)}) copy-start(bf16[256,224]{0,1:T(8,128)(2,1)} %param.24) | copy-start | bytes 344068
  0.0 27.2 %copy-start.39 = (f32[7,16,128]{2,1,0:T(8,128)S(1)}, f32[7,16,128]{2,1,0:T(8,128)}, u32[]{:S(2)}) copy-start(f32[7,16,128]{2,1,0:T(8,128)} %param.20) | copy-start | bytes 172036
  2.7 25.0 %collective-permute-start = (f32[34,8,1,128]{3,1,2,0:T(8,128)S(1)}, f32[34,8,1,128]{3,1,2,0:T(8,128)S(1)}, u32[]{:S(2)}, u32[]{:S(2)}) collective-permute-start(f32[34,8,1,128]{3,1,2,0:T(8,128)S(1)} %get-tuple-element.88), channel_id=1, source_target_pairs={{0,16},{16,32},{32,48},{48,64},{64,80},{80,96},{96,112},{112,0},{1... | collective-permute-start | bytes 417800 | tf_op jit(solution)/shard_map/ppermute | solution.py:18
  2.7 24.9 %collective-permute-start.1 = (f32[34,8,1,128]{3,1,2,0:T(8,128)S(1)}, f32[34,8,1,128]{3,1,2,0:T(8,128)S(1)}, u32[]{:S(2)}, u32[]{:S(2)}) collective-permute-start(f32[34,8,1,128]{3,1,2,0:T(8,128)S(1)} %get-tuple-element.89), channel_id=1, source_target_pairs={{16,0},{32,16},{48,32},{64,48},{80,64},{96,80},{112,96},{0,112},{1... | collective-permute-start | bytes 417800 | tf_op jit(solution)/shard_map/ppermute | solution.py:19
  4.5 23.0 %copy-start.104 = (pred[8]{0:T(512)(128)(4,1)}, pred[8]{0:T(512)(128)(4,1)S(1)}, u32[]{:S(2)}) copy-start(pred[8]{0:T(512)(128)(4,1)S(1)} %compare_bitcast_fusion) | copy-start | bytes 28
  27.2 63.5 %copy-start.97 = (pred[16]{0:T(512)(128)(4,1)}, pred[16]{0:T(512)(128)(4,1)S(1)}, u32[]{:S(2)}) copy-start(pred[16]{0:T(512)(128)(4,1)S(1)} %compare_and_fusion.3) | copy-start | bytes 52
  27.3 29.4 %copy-start.52 = (f32[1,16,128]{2,1,0:T(8,128)}, f32[1,16,128]{2,1,0:T(8,128)S(1)}, u32[]{:S(2)}) copy-start(f32[1,16,128]{2,1,0:T(8,128)S(1)} %get-tuple-element.63) | copy-start | bytes 24580
  27.3 38.9 %copy-start.84 = (f32[16,128]{1,0:T(8,128)}, f32[16,128]{1,0:T(8,128)S(1)}, u32[]{:S(2)}) copy-start(f32[16,128]{1,0:T(8,128)S(1)} %get-tuple-element.62) | copy-start | bytes 24580
  27.3 29.4 %copy-start.42 = (f32[1,16,128]{2,1,0:T(8,128)}, f32[1,16,128]{2,1,0:T(8,128)S(1)}, u32[]{:S(2)}) copy-start(f32[1,16,128]{2,1,0:T(8,128)S(1)} %get-tuple-element.65) | copy-start | bytes 24580
  27.3 37.8 %copy-start.54 = (f32[16,128]{1,0:T(8,128)}, f32[16,128]{1,0:T(8,128)S(1)}, u32[]{:S(2)}) copy-start(f32[16,128]{1,0:T(8,128)S(1)} %get-tuple-element.64) | copy-start | bytes 24580
  27.3 29.4 %copy-start.44 = (f32[1,16,128]{2,1,0:T(8,128)}, f32[1,16,128]{2,1,0:T(8,128)S(1)}, u32[]{:S(2)}) copy-start(f32[1,16,128]{2,1,0:T(8,128)S(1)} %get-tuple-element.67) | copy-start | bytes 24580
  27.4 29.4 %copy-start.64 = (f32[16,128]{1,0:T(8,128)}, f32[16,128]{1,0:T(8,128)S(1)}, u32[]{:S(2)}) copy-start(f32[16,128]{1,0:T(8,128)S(1)} %get-tuple-element.95) | copy-start | bytes 24580
  27.4 29.4 %copy-start.66 = (f32[16,128]{1,0:T(8,128)}, f32[16,128]{1,0:T(8,128)S(1)}, u32[]{:S(2)}) copy-start(f32[16,128]{1,0:T(8,128)S(1)} %get-tuple-element.96) | copy-start | bytes 24580
  27.4 29.4 %copy-start.68 = (f32[16,128]{1,0:T(8,128)}, f32[16,128]{1,0:T(8,128)S(1)}, u32[]{:S(2)}) copy-start(f32[16,128]{1,0:T(8,128)S(1)} %get-tuple-element.97) | copy-start | bytes 24580
  27.4 29.4 %copy-start.70 = (f32[16,128]{1,0:T(8,128)}, f32[16,128]{1,0:T(8,128)S(1)}, u32[]{:S(2)}) copy-start(f32[16,128]{1,0:T(8,128)S(1)} %get-tuple-element.98) | copy-start | bytes 24580
  27.4 29.4 %copy-start.72 = (f32[16,128]{1,0:T(8,128)}, f32[16,128]{1,0:T(8,128)S(1)}, u32[]{:S(2)}) copy-start(f32[16,128]{1,0:T(8,128)S(1)} %get-tuple-element.99) | copy-start | bytes 24580
  27.4 29.4 %copy-start.74 = (f32[16,128]{1,0:T(8,128)}, f32[16,128]{1,0:T(8,128)S(1)}, u32[]{:S(2)}) copy-start(f32[16,128]{1,0:T(8,128)S(1)} %get-tuple-element.100) | copy-start | bytes 24580
  27.4 29.4 %copy-start.76 = (f32[16,128]{1,0:T(8,128)}, f32[16,128]{1,0:T(8,128)S(1)}, u32[]{:S(2)}) copy-start(f32[16,128]{1,0:T(8,128)S(1)} %get-tuple-element.101) | copy-start | bytes 24580
  27.4 29.4 %copy-start.78 = (f32[16,128]{1,0:T(8,128)}, f32[16,128]{1,0:T(8,128)S(1)}, u32[]{:S(2)}) copy-start(f32[16,128]{1,0:T(8,128)S(1)} %get-tuple-element.102) | copy-start | bytes 24580
  27.4 36.6 %copy-start.58 = (f32[16,128]{1,0:T(8,128)}, f32[16,128]{1,0:T(8,128)S(1)}, u32[]{:S(2)}) copy-start(f32[16,128]{1,0:T(8,128)S(1)} %get-tuple-element.66) | copy-start | bytes 24580
  27.4 39.9 %copy-start.56 = (f32[16,128]{1,0:T(8,128)}, f32[16,128]{1,0:T(8,128)S(1)}, u32[]{:S(2)}) copy-start(f32[16,128]{1,0:T(8,128)S(1)} %get-tuple-element.94) | copy-start | bytes 24580
  27.5 29.3 %copy-start.46 = (f32[1,16,128]{2,1,0:T(8,128)}, f32[1,16,128]{2,1,0:T(8,128)S(1)}, u32[]{:S(2)}) copy-start(f32[1,16,128]{2,1,0:T(8,128)S(1)} %get-tuple-element.69) | copy-start | bytes 24580
  27.5 35.5 %copy-start.60 = (f32[16,128]{1,0:T(8,128)}, f32[16,128]{1,0:T(8,128)S(1)}, u32[]{:S(2)}) copy-start(f32[16,128]{1,0:T(8,128)S(1)} %get-tuple-element.68) | copy-start | bytes 24580
  27.5 29.3 %copy-start.48 = (f32[1,16,128]{2,1,0:T(8,128)}, f32[1,16,128]{2,1,0:T(8,128)S(1)}, u32[]{:S(2)}) copy-start(f32[1,16,128]{2,1,0:T(8,128)S(1)} %get-tuple-element.71) | copy-start | bytes 24580
  27.5 34.4 %copy-start.62 = (f32[16,128]{1,0:T(8,128)}, f32[16,128]{1,0:T(8,128)S(1)}, u32[]{:S(2)}) copy-start(f32[16,128]{1,0:T(8,128)S(1)} %get-tuple-element.70) | copy-start | bytes 24580
  27.6 29.3 %copy-start.50 = (f32[1,16,128]{2,1,0:T(8,128)}, f32[1,16,128]{2,1,0:T(8,128)S(1)}, u32[]{:S(2)}) copy-start(f32[1,16,128]{2,1,0:T(8,128)S(1)} %get-tuple-element.73) | copy-start | bytes 24580
  27.6 32.5 %copy-start.80 = (f32[16,128]{1,0:T(8,128)}, f32[16,128]{1,0:T(8,128)S(1)}, u32[]{:S(2)}) copy-start(f32[16,128]{1,0:T(8,128)S(1)} %get-tuple-element.72) | copy-start | bytes 24580
  27.6 29.2 %copy-start.82 = (f32[16,128]{1,0:T(8,128)}, f32[16,128]{1,0:T(8,128)S(1)}, u32[]{:S(2)}) copy-start(f32[16,128]{1,0:T(8,128)S(1)} %add_bitcast_fusion) | copy-start | bytes 24580
  27.7 62.4 %copy-start.92 = (s32[1024]{0:T(1024)}, s32[1024]{0:T(1024)S(1)}, u32[]{:S(2)}) copy-start(s32[1024]{0:T(1024)S(1)} %pad_clamp_fusion.2) | copy-start | bytes 12292
  33.8 10.1 %collective-permute-start.2 = (f32[34,8,18,1]{0,1,3,2:T(8,128)S(1)}, f32[34,8,18,1]{0,1,3,2:T(8,128)S(1)}, u32[]{:S(2)}, u32[]{:S(2)}) collective-permute-start(f32[34,8,18,1]{0,1,3,2:T(8,128)S(1)} %copy.255), channel_id=1, source_target_pairs={{0,1},{1,2},{2,3},{3,4},{4,5},{5,6},{6,7},{7,8},{8,9},{9,10},{10,1... | collective-permute-start | bytes 58760 | tf_op jit(solution)/shard_map/ppermute | solution.py:18
  37.4 9.1 %collective-permute-start.3 = (f32[34,8,18,1]{0,1,3,2:T(8,128)S(1)}, f32[34,8,18,1]{0,1,3,2:T(8,128)S(1)}, u32[]{:S(2)}, u32[]{:S(2)}) collective-permute-start(f32[34,8,18,1]{0,1,3,2:T(8,128)S(1)} %copy.259), channel_id=1, source_target_pairs={{1,0},{2,1},{3,2},{4,3},{5,4},{6,5},{7,6},{8,7},{9,8},{10,9},{11,1... | collective-permute-start | bytes 58760 | tf_op jit(solution)/shard_map/ppermute | solution.py:19
  90.7 32.0 %copy-start.40 = (bf16[224,32]{0,1:T(8,128)(2,1)S(1)}, bf16[224,32]{0,1:T(8,128)(2,1)}, u32[]{:S(2)}) copy-start(bf16[224,32]{0,1:T(8,128)(2,1)} %param.22) | copy-start | bytes 43012
  92.3 29.8 %all-to-all-start = ((bf16[16,1,32,2048]{3,2,1,0:T(8,128)(2,1)}), bf16[16,1,32,2048]{3,2,1,0:T(8,128)(2,1)S(1)}, u32[]{:S(2)}, u32[]{:S(2)}) async-start(bf16[16,1,32,2048]{3,2,1,0:T(8,128)(2,1)} %select_bitcast_fusion.1), calls=%async_computation | async-start | bytes 4194304 | tf_op jit(solution)/shard_map/all_to_all | solution.py:160
  98.5 53.4 %copy-start.90 = (pred[6]{0:T(512)(128)(4,1)}, pred[6]{0:T(512)(128)(4,1)S(1)}, u32[]{:S(2)}) copy-start(pred[6]{0:T(512)(128)(4,1)S(1)} %get-tuple-element.35) | copy-start | bytes 22
  98.5 84.6 %copy-start.95 = (s32[6]{0:T(128)}, s32[6]{0:T(128)S(1)}, u32[]{:S(2)}) copy-start(s32[6]{0:T(128)S(1)} %get-tuple-element.36) | copy-start | bytes 76
  98.5 24.3 %copy-start.94 = (s32[1024]{0:T(1024)}, s32[1024]{0:T(1024)S(1)}, u32[]{:S(2)}) copy-start(s32[1024]{0:T(1024)S(1)} %pad_clamp_fusion.1) | copy-start | bytes 12292
  133.4 14.9 %copy-start.41 = (bf16[32,224]{1,0:T(8,128)(2,1)S(1)}, bf16[32,224]{1,0:T(8,128)(2,1)}, u32[]{:S(2)}) copy-start(bf16[32,224]{1,0:T(8,128)(2,1)} %param.26) | copy-start | bytes 43012
  185.9 29.4 %all-to-all-start.1 = ((bf16[16,1,32,2048]{3,2,1,0:T(8,128)(2,1)}), bf16[16,1,32,2048]{3,2,1,0:T(8,128)(2,1)S(1)}, u32[]{:S(2)}, u32[]{:S(2)}) async-start(bf16[16,1,32,2048]{3,2,1,0:T(8,128)(2,1)} %bitcast.61), calls=%async_computation.1 | async-start | bytes 4194304 | tf_op jit(solution)/shard_map/all_to_all | solution.py:166
  190.4 45.0 %copy-start.100 = (pred[128]{0:T(512)(128)(4,1)}, pred[128]{0:T(512)(128)(4,1)S(1)}, u32[]{:S(2)}) copy-start(pred[128]{0:T(512)(128)(4,1)S(1)} %gt.19) | copy-start | bytes 388
  190.4 25.7 %copy-start.93 = (s32[1024]{0:T(1024)}, s32[1024]{0:T(1024)S(1)}, u32[]{:S(2)}) copy-start(s32[1024]{0:T(1024)S(1)} %pad_clamp_fusion) | copy-start | bytes 12292
  190.4 25.7 %copy-start.102 = (pred[8]{0:T(512)(128)(4,1)}, pred[8]{0:T(512)(128)(4,1)S(1)}, u32[]{:S(2)}) copy-start(pred[8]{0:T(512)(128)(4,1)S(1)} %compare_and_fusion.1) | copy-start | bytes 28
  237.9 4.5 collective-permute-start.4
  237.9 4.5 collective-permute-start.5
  248.5 10.1 %collective-permute-start.6 = (f32[34,8,18,1]{0,1,3,2:T(8,128)S(1)}, f32[34,8,18,1]{0,1,3,2:T(8,128)S(1)}, u32[]{:S(2)}, u32[]{:S(2)}) collective-permute-start(f32[34,8,18,1]{0,1,3,2:T(8,128)S(1)} %copy.284), channel_id=1, source_target_pairs={{0,1},{1,2},{2,3},{3,4},{4,5},{5,6},{6,7},{7,8},{8,9},{9,10},{10,1... | collective-permute-start | bytes 58760 | tf_op jit(solution)/shard_map/ppermute | solution.py:18
  252.5 8.7 %collective-permute-start.7 = (f32[34,8,18,1]{0,1,3,2:T(8,128)S(1)}, f32[34,8,18,1]{0,1,3,2:T(8,128)S(1)}, u32[]{:S(2)}, u32[]{:S(2)}) collective-permute-start(f32[34,8,18,1]{0,1,3,2:T(8,128)S(1)} %copy.288), channel_id=1, source_target_pairs={{1,0},{2,1},{3,2},{4,3},{5,4},{6,5},{7,6},{8,7},{9,8},{10,9},{11,1... | collective-permute-start | bytes 58760 | tf_op jit(solution)/shard_map/ppermute | solution.py:19
  307.2 35.9 %copy-start.91 = (pred[6]{0:T(512)(128)(4,1)S(1)}, pred[6]{0:T(512)(128)(4,1)}, u32[]{:S(2)}) copy-start(pred[6]{0:T(512)(128)(4,1)} %copy-done.90) | copy-start | bytes 22
  406.1 38.0 %all-to-all-start.3 = ((bf16[16,1,32,2048]{3,2,1,0:T(8,128)(2,1)}), bf16[16,1,32,2048]{3,2,1,0:T(8,128)(2,1)S(1)}, u32[]{:S(2)}, u32[]{:S(2)}) async-start(bf16[16,1,32,2048]{3,2,1,0:T(8,128)(2,1)} %bitcast.92), calls=%async_computation.3 | async-start | bytes 4194304 | tf_op jit(solution)/shard_map/all_to_all | solution.py:166
  410.3 34.5 %copy-start.103 = (pred[8]{0:T(512)(128)(4,1)S(1)}, pred[8]{0:T(512)(128)(4,1)}, u32[]{:S(2)}) copy-start(pred[8]{0:T(512)(128)(4,1)} %copy-done.102) | copy-start | bytes 28
  (72 other events, 246.5 us)
where the time goes:
time: 475 us; the launch traced here: 467 us
  local copies, waits for them, and re-layouts  161 us (34%)
  matrix products  107 us (23%)
  waiting for transfers between devices  72.4 us (15%)
  blocking collectives  52.8 us (11%)
  other arithmetic  43.6 us (9%)
  starting transfers between devices  27.7 us (6%)
    dot_general x4, matrix products, react_all(): jnp.einsum('pr,brc->bpc', stoich, rate_values, preferred_element_type=jnp...  59.5 us
    all_to_all x2, waiting for transfers between devices, on_device(): lax.all_to_all(increments.reshape(lon_devices, capacity, n_species, block...  46 us
    unnamed x237, local copies, waits for them, and re-layouts  38 us
    convert_element_type x6, local copies, waits for them, and re-layouts, on_device(): tile_increment.astype(jnp.float32)  37.5 us
    all_to_all x1, blocking collectives, on_device(): lax.all_to_all(outgoing, 'lon', split_axis=0, concat_axis=0, tiled=True)  35.1 us
    dot_general x4, matrix products, react_all(): jnp.einsum('rp,bpc->brc', react_b, species, preferred_element_type=jnp.fl...  25.9 us
    all_to_all x1, waiting for transfers between devices, on_device(): lax.all_to_all(outgoing, 'lon', split_axis=0, concat_axis=0, tiled=True)  23.6 us
    unnamed x1, blocking collectives  17.7 us
  transfers between devices with their start and end apart: 11, of which 4 were waited for; matrix products, arithmetic and copies ran while one was open for 7% of the time, Pallas kernels for 0%

commit v1 on v0

v1 whole, which is shorter than its diff:
```python
import jax
import jax.numpy as jnp
from jax import lax
from jax.experimental import pallas as pl
from jax.experimental.pallas import tpu as pltpu
from jax.sharding import PartitionSpec as P

S = 32
LEV = 8
ROWS = 16
COLS = 128
BLOCK = 16
JOBS = ROWS // 2
FIRST = 11
F32 = jnp.float32
BF16 = jnp.bfloat16
MESH = pl.DeviceIdType.MESH


def dot(a, b):
    return jnp.dot(a, b, preferred_element_type=F32)


def kernel(
    x_hbm, ce_hbm, cn_hbm, mix_hbm, sun_hbm, dec_hbm, ra_hbm, rb_hbm, st_hbm, en_hbm, rc_hbm,
    out_hbm,
    X, da, db, w0, ep, em, epm, nps, nms, lower, upper, inv,
    ce, cn, mix, sun, mask, dec, ra, rb, st, en, rc, aw, bw, ew,
    packed, west, east, halo, to_north, to_south,
    row_sem, small_sem, weight_sem, out_sem, send_sem, recv_sem,
):
    n_lat, n_lon = lax.axis_size("lat"), lax.axis_size("lon")
    lat, lon = lax.axis_index("lat"), lax.axis_index("lon")
    north, south = {"lat": lax.rem(lat + 1, n_lat)}, {"lat": lax.rem(lat + n_lat - 1, n_lat)}
    right, left = {"lon": lax.rem(lon + 1, n_lon)}, {"lon": lax.rem(lon + n_lon - 1, n_lon)}

    barrier = pltpu.get_barrier_semaphore()
    for neighbour in (north, south, right, left):
        pl.semaphore_signal(barrier, inc=1, device_id=neighbour, device_id_type=MESH)

    small = [
        pltpu.make_async_copy(a, b, small_sem.at[i])
        for i, (a, b) in enumerate(((ce_hbm, ce), (cn_hbm, cn), (mix_hbm, mix), (sun_hbm, sun)))
    ]
    weights = [
        pltpu.make_async_copy(a, b, weight_sem.at[i])
        for i, (a, b) in enumerate(
            ((dec_hbm, dec), (ra_hbm, ra), (rb_hbm, rb), (st_hbm, st), (en_hbm, en), (rc_hbm, rc))
        )
    ]
    for copy in small:
        copy.start()

    def load_rows(i, carry):
        r, l = lax.rem(i // LEV + ROWS - 1, ROWS), lax.rem(i, LEV)
        pltpu.make_async_copy(x_hbm.at[:, l, r, :], X.at[0, r + 1, l], row_sem.at[r]).start()
        return carry

    lax.fori_loop(0, ROWS * LEV, load_rows, 0)
    for copy in weights:
        copy.start()

    def wait_row(r):
        pltpu.make_async_copy(da.at[0], X.at[0, r + 1], row_sem.at[r]).wait()

    for copy in small:
        copy.wait()
    lane = lax.broadcasted_iota(jnp.int32, (ROWS, COLS), 1)
    row = lax.broadcasted_iota(jnp.int32, (ROWS, COLS), 0)
    grid_row = row + lat * ROWS
    open_north, open_south = grid_row < n_lat * ROWS - 1, grid_row > 0
    for l in range(LEV):
        c, n = ce[l], cn[l]
        e_plus, e_minus = jnp.maximum(c, 0.0), jnp.minimum(c, 0.0)
        n_plus = jnp.where(open_north, jnp.maximum(n, 0.0), 0.0)
        n_minus = jnp.where(open_south, jnp.minimum(n, 0.0), 0.0)
        ep[l], em[l] = e_plus, e_minus
        epm[l] = jnp.where(lane == COLS - 1, e_plus, e_minus)
        w0[l] = 1.0 - (e_plus - e_minus) - (n_plus - n_minus)
        nps[l] = jnp.where(row == 0, 1.0, pltpu.roll(n_plus, 1, 0))
        nms[l] = jnp.where(row == ROWS - 1, 1.0, pltpu.roll(n_minus, ROWS - 1, 0))
        if l == 0:
            south_factor = n_minus[0:1]
            north_factor = n_plus[ROWS - 1 :]
            factors = [(north_factor, south_factor)]
        else:
            factors.append((n_plus[ROWS - 1 :], n_minus[0:1]))

    wait_row(ROWS - 1)
    wait_row(0)
    for l in range(LEV):
        to_north[0, l] = X[0, ROWS, l] * factors[l][0]
        to_south[0, l] = X[0, 1, l] * factors[l][1]
    pl.semaphore_wait(barrier, 4)

    def edge_copies(step):
        return (
            pltpu.make_async_remote_copy(
                src_ref=to_north.at[step], dst_ref=X.at[step, 0],
                send_sem=send_sem.at[step, 0], recv_sem=recv_sem.at[step, 0],
                device_id=north, device_id_type=MESH,
            ),
            pltpu.make_async_remote_copy(
                src_ref=to_south.at[step], dst_ref=X.at[step, ROWS + 1],
                send_sem=send_sem.at[step, 1], recv_sem=recv_sem.at[step, 1],
                device_id=south, device_id_type=MESH,
            ),
        )

    def side_copies(step, group):
        return (
            pltpu.make_async_remote_copy(
                src_ref=packed.at[step, group], dst_ref=west.at[step, group],
                send_sem=send_sem.at[step, 2 + 2 * group], recv_sem=recv_sem.at[step, 2 + 2 * group],
                device_id=right, device_id_type=MESH,
            ),
            pltpu.make_async_remote_copy(
                src_ref=packed.at[step, group], dst_ref=east.at[step, group],
                send_sem=send_sem.at[step, 3 + 2 * group], recv_sem=recv_sem.at[step, 3 + 2 * group],
                device_id=left, device_id_type=MESH,
            ),
        )

    for copy in edge_copies(0):
        copy.start()

    wide_lane = lax.broadcasted_iota(jnp.int32, (S, COLS), 1)

    def place(r):
        at = lax.rem(r + ROWS - FIRST, ROWS)
        return at // LEV, lax.rem(at, LEV)

    def pack_row(values, r, slot_step):
        group, slot = place(r)
        line = jnp.zeros((S, COLS), F32)
        for l in range(LEV):
            z = values[l] * epm[l, pl.ds(r, 1), :]
            line = jnp.where(wide_lane // 2 == l, pltpu.roll(z, 2 * l + 1, 1), line)
        line = pltpu.roll(line, 16 * slot, 1)
        packed[slot_step, group] = jnp.where(
            wide_lane // 16 == slot, line, packed[slot_step, group]
        )

    packed[...] = jnp.zeros_like(packed)

    def first_pack(i, carry):
        r = lax.rem(i + FIRST, ROWS)

        @pl.when((r > 0) & (r < ROWS - 1))
        def _():
            wait_row(r)

        pack_row([X[0, r + 1, l] for l in range(LEV)], r, 0)
        return carry

    for group in range(2):
        lax.fori_loop(group * 8, group * 8 + 8, first_pack, 0)
        for copy in side_copies(0, group):
            copy.start()

    pivot_upper = None
    for l in range(LEV):
        below = mix[l - 1] if l > 0 else None
        above = mix[l] if l < LEV - 1 else None
        pivot = 1.0
        if below is not None:
            pivot = pivot + below
        if above is not None:
            pivot = pivot + above
        if below is not None:
            pivot = pivot - below * pivot_upper
            lower[l] = below
        recip = 1.0 / pivot
        inv[l] = recip
        if above is not None:
            pivot_upper = above * recip
            upper[l] = pivot_upper
    block = lax.broadcasted_iota(jnp.int32, (1, COLS), 1) // BLOCK
    lit = jnp.zeros((1, COLS), jnp.int32)
    for b in range(COLS // BLOCK):
        lit = jnp.where(block == b, sun[0:1, b : b + 1], lit)
    mask[...] = lit
    for copy in weights:
        copy.wait()
    aw[...] = dot(ra[...], dec[...]).astype(BF16)
    bw[...] = dot(rb[...], dec[...]).astype(BF16)
    ew[...] = (dot(en[...], st[...]) * rc[...]).astype(BF16)

    def unpack(step, group):
        halo[step, group] = jnp.where(
            lax.rem(wide_lane, 2) == 0,
            pltpu.roll(east[step, group], COLS - 1, 1),
            pltpu.roll(west[step, group], 1, 1),
        )

    def transport(job, dest):
        step, turn = job // JOBS, lax.rem(job, JOBS)
        for k in range(2):
            r = lax.rem(2 * turn + FIRST + 2 * step + k, ROWS)
            group, slot = place(r)
            line = pltpu.roll(halo[step, group], lax.rem(COLS - 16 * slot, COLS), 1)
            solved = []
            for l in range(LEV):
                at = lambda ref: ref[l, pl.ds(r, 1), :]
                q = X[step, r + 1, l]
                side = pltpu.roll(line, COLS - (2 * l + 1), 1)
                from_west = jnp.where(wide_lane == 0, side, pltpu.roll(q * at(ep), 1, 1))
                from_east = jnp.where(
                    wide_lane == COLS - 1, side, pltpu.roll(q * at(em), COLS - 1, 1)
                )
                value = (
                    q * at(w0)
                    + (from_west - from_east)
                    + (X[step, r, l] * at(nps) - X[step, r + 2, l] * at(nms))
                )
                if l > 0:
                    value = value + at(lower) * solved[-1]
                solved.append(value * at(inv))
            value = solved[-1]
            dest[k, LEV - 1] = value
            for l in range(LEV - 2, -1, -1):
                value = solved[l] + upper[l, pl.ds(r, 1), :] * value
                dest[k, l] = value

    def chemistry(job, source):
        step, turn = job // JOBS, lax.rem(job, JOBS)
        current = jnp.concatenate([source[k, l] for k in range(2) for l in range(LEV)], axis=1)
        summed = None
        for substep in range(2):
            lines = current.astype(BF16)
            rates = (dot(aw[...], lines) * dot(bw[...], lines)).astype(BF16)
            change = dot(ew[...], rates)
            summed = change if summed is None else summed + change
            current = current + change
        lit_lanes = jnp.broadcast_to(mask[...], (S, COLS)) > 0
        for k in range(2):
            r = lax.rem(2 * turn + FIRST + 2 * step + k, ROWS)
            values = []
            for l in range(LEV):
                at = (k * LEV + l) * COLS
                value = source[k, l] + jnp.where(lit_lanes, summed[:, at : at + COLS], 0.0)
                X[step + 1, r + 1, l] = value
                values.append(value)
            pack_row(values, r, step + 1)

    def after(job):
        @pl.when(job == 2)
        def _():
            for l in range(LEV):
                to_north[1, l] = X[1, ROWS, l] * jnp.where(
                    lat < n_lat - 1, jnp.maximum(cn[l, ROWS - 1 :, :], 0.0), 0.0
                )
                to_south[1, l] = X[1, 1, l] * jnp.where(
                    lat > 0, jnp.minimum(cn[l, 0:1, :], 0.0), 0.0
                )
            for copy in edge_copies(1):
                copy.start()

        for group in range(2):

            @pl.when(job == 3 + 4 * group)
            def _():
                for copy in side_copies(1, group):
                    copy.start()

        @pl.when(job >= JOBS)
        def _():
            def store(i, carry):
                r = lax.rem(2 * (job - JOBS) + FIRST + 2 + i // LEV, ROWS)
                l = lax.rem(i, LEV)
                pltpu.make_async_copy(X.at[2, r + 1, l], out_hbm.at[:, l, r, :], out_sem).start()
                return carry

            lax.fori_loop(0, 2 * LEV, store, 0)

    def before(job):
        @pl.when(job == JOBS - 1)
        def _():
            for copy in edge_copies(1):
                copy.wait()
            for copy in side_copies(1, 0):
                copy.wait()
            unpack(1, 0)

        @pl.when(job == JOBS + 2)
        def _():
            for copy in side_copies(1, 1):
                copy.wait()
            unpack(1, 1)

    for copy in edge_copies(0):
        copy.wait()
    for group in range(2):
        for copy in side_copies(0, group):
            copy.wait()
        unpack(0, group)
    transport(0, da)

    def pair(i, carry):
        for k, (here, there) in enumerate(((da, db), (db, da))):
            job = 2 * i + k
            before(job)
            transport(jnp.minimum(job + 1, 2 * JOBS - 1), there)
            chemistry(job, here)
            after(job)
        return carry

    lax.fori_loop(0, JOBS, pair, 0)
    pltpu.make_async_copy(X.at[0, 1 : ROWS + 1], X.at[2, 1 : ROWS + 1], out_sem).wait()


def on_device(latent_field, east_courant, north_courant, mixing, sunlit, decode_w, react_a, react_b, stoich, encode_w, rate_const):
    coefficient = pltpu.VMEM((LEV, ROWS, COLS), F32)
    tile = pltpu.VMEM((2, LEV, S, COLS), F32)
    n_species, n_reactions = stoich.shape
    return pl.pallas_call(
        kernel,
        name="split_steps",
        out_shape=jax.ShapeDtypeStruct(latent_field.shape, F32),
        in_specs=[pl.BlockSpec(memory_space=pl.ANY)] * 11,
        out_specs=pl.BlockSpec(memory_space=pl.ANY),
        scratch_shapes=[
            pltpu.VMEM((3, ROWS + 2, LEV, S, COLS), F32), tile, tile,
            coefficient, coefficient, coefficient, coefficient, coefficient, coefficient,
            coefficient, coefficient, coefficient,
            coefficient, coefficient, pltpu.VMEM((LEV - 1, ROWS, COLS), F32),
            pltpu.VMEM((1, COLS // BLOCK), jnp.int32), pltpu.VMEM((1, COLS), jnp.int32),
            pltpu.VMEM((n_species, S), BF16),
            pltpu.VMEM((n_reactions, n_species), BF16), pltpu.VMEM((n_reactions, n_species), BF16),
            pltpu.VMEM((n_species, n_reactions), BF16), pltpu.VMEM((S, n_species), BF16),
            pltpu.VMEM((1, n_reactions), F32),
            pltpu.VMEM((n_reactions, S), BF16), pltpu.VMEM((n_reactions, S), BF16),
            pltpu.VMEM((S, n_reactions), BF16),
            pltpu.VMEM((3, 2, S, COLS), F32), pltpu.VMEM((2, 2, S, COLS), F32),
            pltpu.VMEM((2, 2, S, COLS), F32), pltpu.VMEM((2, 2, S, COLS), F32),
            pltpu.VMEM((2, LEV, S, COLS), F32), pltpu.VMEM((2, LEV, S, COLS), F32),
            pltpu.SemaphoreType.DMA((ROWS,)), pltpu.SemaphoreType.DMA((4,)),
            pltpu.SemaphoreType.DMA((6,)), pltpu.SemaphoreType.DMA,
            pltpu.SemaphoreType.DMA((2, 6)), pltpu.SemaphoreType.DMA((2, 6)),
        ],
        compiler_params=pltpu.CompilerParams(
            collective_id=0, has_side_effects=True, vmem_limit_bytes=48 << 20
        ),
    )(
        latent_field, east_courant, north_courant, mixing, sunlit, decode_w, react_a, react_b,
        stoich, encode_w, rate_const.reshape(1, -1),
    )


def solution(mesh):
    placed = (
        P(None, None, "lat", "lon"),
        P(None, "lat", "lon"),
        P(None, "lat", "lon"),
        P(None, "lat", "lon"),
        P("lat", "lon"),
        P(),
        P(),
        P(),
        P(),
        P(),
        P(),
    )
    return jax.shard_map(
        on_device,
        mesh=mesh,
        in_specs=placed,
        out_specs=P(None, None, "lat", "lon"),
        check_vma=False,
    )
```

time: 475 us -> 60.4 us (0.13); the launches traced: 467 us -> 59.8 us
  local copies, waits for them, and re-layouts: 161 us -> 11.2 us
  matrix products: 107 us -> 0 us
  waiting for transfers between devices: 72.4 us -> 0 us
  blocking collectives: 52.8 us -> 0 us
  Pallas kernels: 0 us -> 48.6 us
  other arithmetic: 43.6 us -> 0 us
  starting transfers between devices: 27.7 us -> 0 us
    dot_general x16 -> x0, matrix products: 107 us -> none  [the longest x4 59.5 us: react_all(): jnp.einsum('pr,brc->bpc', stoich, rate_values, preferred_element_type=jnp...]
    all_to_all x3 -> x0, waiting for transfers between devices: 69.6 us -> none  [the longest x2 46 us: on_device(): lax.all_to_all(increments.reshape(lon_devices, capacity, n_species, block...]
    pallas_call x0 -> x1, Pallas kernels: none -> 48.6 us  [on_device(): pl.pallas_call(kernel, name='split_steps', out_shape=jax.ShapeDtypeStruct...]
    convert_element_type x6 -> x0, local copies, waits for them, and re-layouts: 37.5 us -> none  [on_device(): tile_increment.astype(jnp.float32)]
    all_to_all x1 -> x0, blocking collectives: 35.1 us -> none  [on_device(): lax.all_to_all(outgoing, 'lon', split_axis=0, concat_axis=0, tiled=True)]
    another operation x23 -> x0, local copies, waits for them, and re-layouts: 27.8 us -> none  [the longest x4 14.2 us: diffuse(): return jnp.stack(solved, 1)]
    unnamed x237 -> x20, local copies, waits for them, and re-layouts: 38 us -> 11.2 us
    unnamed x1 -> x0, blocking collectives: 17.7 us -> none
  transfers between devices with their start and end apart: 11 -> 0, of which waited for: 4 -> 0; matrix products, arithmetic and copies ran while one was open for 7% -> 0% of each run, Pallas kernels for 0% -> 0%
where the time goes in v1:
time: 60.4 us; the launch traced here: 59.8 us
  Pallas kernels  48.6 us (80%)
  local copies, waits for them, and re-layouts  11.2 us (19%)
    pallas_call x1, Pallas kernels, on_device(): pl.pallas_call(kernel, name='split_steps', out_shape=jax.ShapeDtypeStruct...  48.6 us
    unnamed x20, local copies, waits for them, and re-layouts  11.2 us

profile of v1, /device:TPU:6, one launch (start us, length us, event | category | flops | bytes accessed | tf_op | source)
XLA Modules:
  0.0 59.8 jit_solution(7691325802691648705)
XLA Ops:
  0.0 0.8 %copy.12.dec_hbm = bf16[224,32]{1,0:T(8,128)(2,1)S(1)} copy(bf16[224,32]{0,1:T(8,128)(2,1)} %param.16) | data formatting | bytes 28672 | tf_op args[5]
  0.8 1.0 %copy.13.ra_hbm = bf16[256,224]{1,0:T(8,128)(2,1)S(1)} copy(bf16[256,224]{0,1:T(8,128)(2,1)} %param.17) | data formatting | bytes 229376 | tf_op args[6]
  1.8 1.0 %copy.14.rb_hbm = bf16[256,224]{1,0:T(8,128)(2,1)S(1)} copy(bf16[256,224]{0,1:T(8,128)(2,1)} %param.18) | data formatting | bytes 229376 | tf_op args[7]
  2.8 0.0 copy-start
  2.9 1.6 %copy-done = f32[32,8,16,128]{3,2,1,0:T(8,128)S(1)} copy-done((f32[32,8,16,128]{3,2,1,0:T(8,128)S(1)}, f32[32,8,16,128]{3,2,1,0:T(8,128)}, u32[]{:S(2)}) %copy-start) | copy-done | bytes 2097176
  4.4 0.0 copy-start.1
  4.4 0.9 %copy-done.1 = bf16[224,256]{1,0:T(8,128)(2,1)S(1)} copy-done((bf16[224,256]{1,0:T(8,128)(2,1)S(1)}, bf16[224,256]{1,0:T(8,128)(2,1)}, u32[]{:S(2)}) %copy-start.1) | copy-done | bytes 114712
  5.3 0.0 copy-start.2
  5.3 0.8 %copy-done.2 = f32[8,16,128]{2,1,0:T(8,128)S(1)} copy-done((f32[8,16,128]{2,1,0:T(8,128)S(1)}, f32[8,16,128]{2,1,0:T(8,128)}, u32[]{:S(2)}) %copy-start.2) | copy-done | bytes 65560
  6.2 0.0 copy-start.3
  6.2 0.8 %copy-done.3 = f32[8,16,128]{2,1,0:T(8,128)S(1)} copy-done((f32[8,16,128]{2,1,0:T(8,128)S(1)}, f32[8,16,128]{2,1,0:T(8,128)}, u32[]{:S(2)}) %copy-start.3) | copy-done | bytes 65560
  7.0 0.0 copy-start.4
  7.0 0.8 %copy-done.4 = f32[7,16,128]{2,1,0:T(8,128)S(1)} copy-done((f32[7,16,128]{2,1,0:T(8,128)S(1)}, f32[7,16,128]{2,1,0:T(8,128)}, u32[]{:S(2)}) %copy-start.4) | copy-done | bytes 57368
  7.8 0.0 copy-start.5
  7.8 0.7 %copy-done.5 = bf16[32,224]{1,0:T(8,128)(2,1)S(1)} copy-done((bf16[32,224]{1,0:T(8,128)(2,1)S(1)}, bf16[32,224]{1,0:T(8,128)(2,1)}, u32[]{:S(2)}) %copy-start.5) | copy-done | bytes 14360
  8.6 0.0 copy-start.6
  8.6 0.7 %copy-done.6 = f32[256]{0:T(256)S(1)} copy-done((f32[256]{0:T(256)S(1)}, f32[256]{0:T(256)}, u32[]{:S(2)}) %copy-start.6) | copy-done | bytes 1048
  9.2 0.0 copy-start.7
  9.2 0.7 %copy-done.7 = s32[1,8]{1,0:T(1,128)S(1)} copy-done((s32[1,8]{1,0:T(1,128)S(1)}, s32[1,8]{1,0:T(1,128)}, u32[]{:S(2)}) %copy-start.7) | copy-done | bytes 56
  9.9 48.6 %split_steps.1 = f32[32,8,16,128]{3,2,1,0:T(8,128)S(1)} custom-call(f32[32,8,16,128]{3,2,1,0:T(8,128)S(1)} %copy-done, f32[8,16,128]{2,1,0:T(8,128)S(1)} %copy-done.2, f32[8,16,128]{2,1,0:T(8,128)S(1)} %copy-done.3, f32[7,16,128]{2,1,0:T(8,128)S(1)} %copy-done.4, s32[1,8]{1,0:T(1,128)S(1)} %copy-done.7, bf16[224,32]{1,0:T(8,128)(2,1)S(1)} %copy.12.dec_hbm, ...), custom_call_target="tpu_custom_call" | custom-call | tf_op jit(solution)/shard_map/split_steps/pallas_call | solution.py:316
  58.5 1.3 %copy.16 = f32[32,8,16,128]{3,2,1,0:T(8,128)} copy(f32[32,8,16,128]{3,2,1,0:T(8,128)S(1)} %split_steps.1) | data formatting | bytes 4194304
Async XLA Ops:
  2.8 1.6 %copy-start = (f32[32,8,16,128]{3,2,1,0:T(8,128)S(1)}, f32[32,8,16,128]{3,2,1,0:T(8,128)}, u32[]{:S(2)}) copy-start(f32[32,8,16,128]{3,2,1,0:T(8,128)} %x_hbm.1) | copy-start | bytes 6291460
  4.4 0.9 %copy-start.1 = (bf16[224,256]{1,0:T(8,128)(2,1)S(1)}, bf16[224,256]{1,0:T(8,128)(2,1)}, u32[]{:S(2)}) copy-start(bf16[224,256]{1,0:T(8,128)(2,1)} %st_hbm.1) | copy-start | bytes 344068
  5.3 0.8 %copy-start.2 = (f32[8,16,128]{2,1,0:T(8,128)S(1)}, f32[8,16,128]{2,1,0:T(8,128)}, u32[]{:S(2)}) copy-start(f32[8,16,128]{2,1,0:T(8,128)} %ce_hbm.1) | copy-start | bytes 196612
  6.2 0.8 %copy-start.3 = (f32[8,16,128]{2,1,0:T(8,128)S(1)}, f32[8,16,128]{2,1,0:T(8,128)}, u32[]{:S(2)}) copy-start(f32[8,16,128]{2,1,0:T(8,128)} %cn_hbm.1) | copy-start | bytes 196612
  7.0 0.8 %copy-start.4 = (f32[7,16,128]{2,1,0:T(8,128)S(1)}, f32[7,16,128]{2,1,0:T(8,128)}, u32[]{:S(2)}) copy-start(f32[7,16,128]{2,1,0:T(8,128)} %mix_hbm.1) | copy-start | bytes 172036
  7.8 0.7 %copy-start.5 = (bf16[32,224]{1,0:T(8,128)(2,1)S(1)}, bf16[32,224]{1,0:T(8,128)(2,1)}, u32[]{:S(2)}) copy-start(bf16[32,224]{1,0:T(8,128)(2,1)} %en_hbm.1) | copy-start | bytes 43012
  8.6 0.7 %copy-start.6 = (f32[256]{0:T(256)S(1)}, f32[256]{0:T(256)}, u32[]{:S(2)}) copy-start(f32[256]{0:T(256)} %param.21) | copy-start | bytes 3076
  9.2 0.7 %copy-start.7 = (s32[1,8]{1,0:T(1,128)S(1)}, s32[1,8]{1,0:T(1,128)}, u32[]{:S(2)}) copy-start(s32[1,8]{1,0:T(1,128)} %sun_hbm.1) | copy-start | bytes 100

commit v2 on v1

--- a/solution.py
+++ b/solution.py
@@ -182,8 +182,8 @@
     mask[...] = lit
     for copy in weights:
         copy.wait()
-    aw[...] = dot(ra[...], dec[...]).astype(BF16)
-    bw[...] = dot(rb[...], dec[...]).astype(BF16)
+    aw[...] = dot(dec[...], ra[...]).T.astype(BF16)
+    bw[...] = dot(dec[...], rb[...]).T.astype(BF16)
     ew[...] = (dot(en[...], st[...]) * rc[...]).astype(BF16)
 
     def unpack(step, group):
@@ -325,8 +325,8 @@
             coefficient, coefficient, coefficient,
             coefficient, coefficient, pltpu.VMEM((LEV - 1, ROWS, COLS), F32),
             pltpu.VMEM((1, COLS // BLOCK), jnp.int32), pltpu.VMEM((1, COLS), jnp.int32),
-            pltpu.VMEM((n_species, S), BF16),
-            pltpu.VMEM((n_reactions, n_species), BF16), pltpu.VMEM((n_reactions, n_species), BF16),
+            pltpu.VMEM((S, n_species), BF16),
+            pltpu.VMEM((n_species, n_reactions), BF16), pltpu.VMEM((n_species, n_reactions), BF16),
             pltpu.VMEM((n_species, n_reactions), BF16), pltpu.VMEM((S, n_species), BF16),
             pltpu.VMEM((1, n_reactions), F32),
             pltpu.VMEM((n_reactions, S), BF16), pltpu.VMEM((n_reactions, S), BF16),
@@ -339,11 +339,11 @@
             pltpu.SemaphoreType.DMA((2, 6)), pltpu.SemaphoreType.DMA((2, 6)),
         ],
         compiler_params=pltpu.CompilerParams(
-            collective_id=0, has_side_effects=True, vmem_limit_bytes=48 << 20
+            collective_id=0, has_side_effects=True
         ),
     )(
-        latent_field, east_courant, north_courant, mixing, sunlit, decode_w, react_a, react_b,
-        stoich, encode_w, rate_const.reshape(1, -1),
+        latent_field, east_courant, north_courant, mixing, sunlit, decode_w.T, react_a.T,
+        react_b.T, stoich, encode_w, rate_const.reshape(1, -1),
     )
 
 

time: 60.4 us -> 48.8 us (0.81)
  local copies, waits for them, and re-layouts: 11.2 us -> 3.13 us
  Pallas kernels: 48.6 us -> 45.4 us
    unnamed x20 -> x1, local copies, waits for them, and re-layouts: 11.2 us -> 3.13 us
    pallas_call x1, Pallas kernels: 48.6 us -> 45.4 us  [on_device(): pl.pallas_call(kernel, name='split_steps', out_shape=jax.ShapeDtypeStruct...]
where the time goes in v2:
time: 48.8 us; the launch traced here: 48.5 us
  Pallas kernels  45.4 us (93%)
  local copies, waits for them, and re-layouts  3.13 us (6%)
    pallas_call x1, Pallas kernels, on_device(): pl.pallas_call(kernel, name='split_steps', out_shape=jax.ShapeDtypeStruct...  45.4 us
    unnamed x1, local copies, waits for them, and re-layouts  3.13 us

profile of v2, /device:TPU:6, one launch (start us, length us, event | category | flops | bytes accessed | tf_op | source)
XLA Modules:
  0.0 48.5 jit_solution(7728520954514985159)
XLA Ops:
  0.0 45.4 %split_steps.1 = f32[32,8,16,128]{3,2,1,0:T(8,128)} custom-call(f32[32,8,16,128]{3,2,1,0:T(8,128)} %x_hbm.1, f32[8,16,128]{2,1,0:T(8,128)} %ce_hbm.1, f32[8,16,128]{2,1,0:T(8,128)} %cn_hbm.1, f32[7,16,128]{2,1,0:T(8,128)} %mix_hbm.1, s32[1,8]{1,0:T(1,128)} %sun_hbm.1, bf16[32,224]{1,0:T(8,128)(2,1)} %bitcast.6, bf16[224,256]{1,0:T(8,128)(2,1)} %bitcast.4, ...), custom_call_target="tpu_custom_call" | custom-call | tf_op jit(solution)/shard_map/split_steps/pallas_call | solution.py:316
  45.4 3.1 %copy.13 = f32[32,8,16,128]{3,2,1,0:T(8,128)} copy(f32[32,8,16,128]{3,2,1,0:T(8,128)} %split_steps.1) | data formatting | bytes 4194304

commit v3 on v2

--- a/solution.py
+++ b/solution.py
@@ -21,13 +21,17 @@
     return jnp.dot(a, b, preferred_element_type=F32)
 
 
+def dot_t(a, b):
+    return lax.dot_general(a, b, (((1,), (1,)), ((), ())), preferred_element_type=F32)
+
+
 def kernel(
     x_hbm, ce_hbm, cn_hbm, mix_hbm, sun_hbm, dec_hbm, ra_hbm, rb_hbm, st_hbm, en_hbm, rc_hbm,
-    out_hbm,
-    X, da, db, w0, ep, em, epm, nps, nms, lower, upper, inv,
-    ce, cn, mix, sun, mask, dec, ra, rb, st, en, rc, aw, bw, ew,
+    out,
+    raw, X, da, db, edge, w0, ep, em, epm, nps, nms, lower, upper, inv,
+    ce, cn, mix, sun, mask, dec, ra, rb, st, en, rc, quad, mid,
     packed, west, east, halo, to_north, to_south,
-    row_sem, small_sem, weight_sem, out_sem, send_sem, recv_sem,
+    level_sem, small_sem, weight_sem, send_sem, recv_sem,
 ):
     n_lat, n_lon = lax.axis_size("lat"), lax.axis_size("lon")
     lat, lon = lax.axis_index("lat"), lax.axis_index("lon")
@@ -51,17 +55,13 @@
     for copy in small:
         copy.start()
 
-    def load_rows(i, carry):
-        r, l = lax.rem(i // LEV + ROWS - 1, ROWS), lax.rem(i, LEV)
-        pltpu.make_async_copy(x_hbm.at[:, l, r, :], X.at[0, r + 1, l], row_sem.at[r]).start()
-        return carry
-
-    lax.fori_loop(0, ROWS * LEV, load_rows, 0)
+    def level_copy(l):
+        return pltpu.make_async_copy(x_hbm.at[:, l], raw.at[:, l], level_sem.at[l])
+
+    for l in range(LEV):
+        level_copy(l).start()
     for copy in weights:
         copy.start()
-
-    def wait_row(r):
-        pltpu.make_async_copy(da.at[0], X.at[0, r + 1], row_sem.at[r]).wait()
 
     for copy in small:
         copy.wait()
@@ -79,19 +79,7 @@
         w0[l] = 1.0 - (e_plus - e_minus) - (n_plus - n_minus)
         nps[l] = jnp.where(row == 0, 1.0, pltpu.roll(n_plus, 1, 0))
         nms[l] = jnp.where(row == ROWS - 1, 1.0, pltpu.roll(n_minus, ROWS - 1, 0))
-        if l == 0:
-            south_factor = n_minus[0:1]
-            north_factor = n_plus[ROWS - 1 :]
-            factors = [(north_factor, south_factor)]
-        else:
-            factors.append((n_plus[ROWS - 1 :], n_minus[0:1]))
-
-    wait_row(ROWS - 1)
-    wait_row(0)
-    for l in range(LEV):
-        to_north[0, l] = X[0, ROWS, l] * factors[l][0]
-        to_south[0, l] = X[0, 1, l] * factors[l][1]
-    pl.semaphore_wait(barrier, 4)
+        edge[l, 0:1], edge[l, 1:2] = n_plus[ROWS - 1 :], n_minus[0:1]
 
     def edge_copies(step):
         return (
@@ -121,9 +109,6 @@
             ),
         )
 
-    for copy in edge_copies(0):
-        copy.start()
-
     wide_lane = lax.broadcasted_iota(jnp.int32, (S, COLS), 1)
 
     def place(r):
@@ -143,20 +128,32 @@
 
     packed[...] = jnp.zeros_like(packed)
 
-    def first_pack(i, carry):
-        r = lax.rem(i + FIRST, ROWS)
-
-        @pl.when((r > 0) & (r < ROWS - 1))
-        def _():
-            wait_row(r)
-
-        pack_row([X[0, r + 1, l] for l in range(LEV)], r, 0)
+    def first_level(l, carry):
+        level_copy(l).wait()
+        lines = [packed[0, 0], packed[0, 1]]
+        for half in range(ROWS // 8):
+            parts = [
+                jnp.swapaxes(raw[s : s + 8, l, 8 * half : 8 * half + 8, :], 0, 1)
+                for s in range(0, S, 8)
+            ]
+            for k in range(8):
+                r = 8 * half + k
+                value = jnp.concatenate([part[k] for part in parts], axis=0)
+                X[0, r + 1, l] = value
+                if r == 0:
+                    to_south[0, l] = value * edge[l, 1:2]
+                if r == ROWS - 1:
+                    to_north[0, l] = value * edge[l, 0:1]
+                group, slot = divmod((r + ROWS - FIRST) % ROWS, LEV)
+                moved = pltpu.roll(value * epm[l, r : r + 1, :], 16 * slot + 2 * l + 1, 1)
+                lines[group] = jnp.where(wide_lane // 2 == 8 * slot + l, moved, lines[group])
+        packed[0, 0], packed[0, 1] = lines
         return carry
 
-    for group in range(2):
-        lax.fori_loop(group * 8, group * 8 + 8, first_pack, 0)
-        for copy in side_copies(0, group):
-            copy.start()
+    lax.fori_loop(0, LEV, first_level, 0)
+    pl.semaphore_wait(barrier, 4)
+    for copy in side_copies(0, 0) + edge_copies(0) + side_copies(0, 1):
+        copy.start()
 
     pivot_upper = None
     for l in range(LEV):
@@ -182,9 +179,21 @@
     mask[...] = lit
     for copy in weights:
         copy.wait()
-    aw[...] = dot(dec[...], ra[...]).T.astype(BF16)
-    bw[...] = dot(dec[...], rb[...]).T.astype(BF16)
-    ew[...] = (dot(en[...], st[...]) * rc[...]).astype(BF16)
+    a = dot(dec[...], ra[...])
+    b = dot(dec[...], rb[...])
+    e = dot(en[...], st[...]) * rc[...]
+    pairs = []
+    for d in range(S // 2 + 1):
+        a_on = a if d == 0 else jnp.concatenate([a[d:], a[:d]], axis=0)
+        b_on = b if d == 0 else jnp.concatenate([b[d:], b[:d]], axis=0)
+        pairs.append(a * b_on if d in (0, S // 2) else a * b_on + a_on * b)
+    pairs = jnp.concatenate(pairs, axis=0)
+    pairs_top, e_top = pairs.astype(BF16), e.astype(BF16)
+    pairs_rest = (pairs - pairs_top.astype(F32)).astype(BF16)
+    e_rest = (e - e_top.astype(F32)).astype(BF16)
+    quad[...] = (
+        dot_t(e_top, pairs_top) + (dot_t(e_rest, pairs_top) + dot_t(e_top, pairs_rest))
+    ).astype(BF16)
 
     def unpack(step, group):
         halo[step, group] = jnp.where(
@@ -217,110 +226,133 @@
                     value = value + at(lower) * solved[-1]
                 solved.append(value * at(inv))
             value = solved[-1]
-            dest[k, LEV - 1] = value
+            dest[k, LEV - 1, 0:S] = value
+            dest[k, LEV - 1, S:] = value
             for l in range(LEV - 2, -1, -1):
                 value = solved[l] + upper[l, pl.ds(r, 1), :] * value
-                dest[k, l] = value
-
-    def chemistry(job, source):
-        step, turn = job // JOBS, lax.rem(job, JOBS)
-        current = jnp.concatenate([source[k, l] for k in range(2) for l in range(LEV)], axis=1)
-        summed = None
-        for substep in range(2):
-            lines = current.astype(BF16)
-            rates = (dot(aw[...], lines) * dot(bw[...], lines)).astype(BF16)
-            change = dot(ew[...], rates)
-            summed = change if summed is None else summed + change
-            current = current + change
+                dest[k, l, 0:S] = value
+                dest[k, l, S:] = value
+
+    def products(ref, k, l):
+        shifted = [ref[k, l, 0 : 3 * S // 2]]
+        shifted += [ref[k, l, b : b + S + 8] for b in range(1, 8)]
+        lines = shifted[0][0:S].astype(BF16)
+        return jnp.concatenate(
+            [
+                lines * shifted[d % 8][d // 8 * 8 : d // 8 * 8 + S].astype(BF16)
+                for d in range(S // 2 + 1)
+            ],
+            axis=0,
+        )
+
+    def chemistry(step, job, source):
+        turn = lax.rem(job, JOBS)
         lit_lanes = jnp.broadcast_to(mask[...], (S, COLS)) > 0
+        for k in range(2):
+            for l in range(0, LEV, 2):
+                change = dot(
+                    quad[...],
+                    jnp.concatenate([products(source, k, l), products(source, k, l + 1)], axis=1),
+                )
+                for h in range(2):
+                    value = source[k, l + h, 0:S] + change[:, h * COLS : (h + 1) * COLS]
+                    mid[k, l + h, 0:S] = value
+                    mid[k, l + h, S:] = value
         for k in range(2):
             r = lax.rem(2 * turn + FIRST + 2 * step + k, ROWS)
             values = []
-            for l in range(LEV):
-                at = (k * LEV + l) * COLS
-                value = source[k, l] + jnp.where(lit_lanes, summed[:, at : at + COLS], 0.0)
-                X[step + 1, r + 1, l] = value
-                values.append(value)
-            pack_row(values, r, step + 1)
-
-    def after(job):
-        @pl.when(job == 2)
-        def _():
-            for l in range(LEV):
-                to_north[1, l] = X[1, ROWS, l] * jnp.where(
-                    lat < n_lat - 1, jnp.maximum(cn[l, ROWS - 1 :, :], 0.0), 0.0
+            for l in range(0, LEV, 2):
+                change = dot(
+                    quad[...],
+                    jnp.concatenate([products(mid, k, l), products(mid, k, l + 1)], axis=1),
                 )
-                to_south[1, l] = X[1, 1, l] * jnp.where(
-                    lat > 0, jnp.minimum(cn[l, 0:1, :], 0.0), 0.0
-                )
-            for copy in edge_copies(1):
-                copy.start()
-
-        for group in range(2):
-
-            @pl.when(job == 3 + 4 * group)
-            def _():
-                for copy in side_copies(1, group):
-                    copy.start()
-
-        @pl.when(job >= JOBS)
-        def _():
-            def store(i, carry):
-                r = lax.rem(2 * (job - JOBS) + FIRST + 2 + i // LEV, ROWS)
-                l = lax.rem(i, LEV)
-                pltpu.make_async_copy(X.at[2, r + 1, l], out_hbm.at[:, l, r, :], out_sem).start()
-                return carry
-
-            lax.fori_loop(0, 2 * LEV, store, 0)
-
-    def before(job):
-        @pl.when(job == JOBS - 1)
-        def _():
-            for copy in edge_copies(1):
-                copy.wait()
-            for copy in side_copies(1, 0):
-                copy.wait()
-            unpack(1, 0)
-
-        @pl.when(job == JOBS + 2)
-        def _():
-            for copy in side_copies(1, 1):
-                copy.wait()
-            unpack(1, 1)
-
-    for copy in edge_copies(0):
-        copy.wait()
-    for group in range(2):
-        for copy in side_copies(0, group):
+                for h in range(2):
+                    value = jnp.where(
+                        lit_lanes,
+                        mid[k, l + h, 0:S] + change[:, h * COLS : (h + 1) * COLS],
+                        source[k, l + h, 0:S],
+                    )
+                    X[step + 1, r + 1, l + h] = value
+                    values.append(value)
+            if step == 0:
+                pack_row(values, r, 1)
+
+    def send_edges():
+        for l in range(LEV):
+            to_north[1, l] = X[1, ROWS, l] * edge[l, 0:1]
+            to_south[1, l] = X[1, 1, l] * edge[l, 1:2]
+        for copy in edge_copies(1):
+            copy.start()
+
+    def send_sides(group):
+        for copy in side_copies(1, group):
+            copy.start()
+
+    def wait_second():
+        wait_edges(1)
+        wait_sides(1, 0)
+
+    def wait_edges(step):
+        for copy in edge_copies(step):
             copy.wait()
-        unpack(0, group)
+
+    def wait_sides(step, group):
+        for copy in side_copies(step, group):
+            copy.wait()
+        unpack(step, group)
+
+    ahead = {
+        1: lambda: wait_edges(0),
+        3: lambda: wait_sides(0, 1),
+        JOBS - 1: wait_second,
+        JOBS + 2: lambda: wait_sides(1, 1),
+    }
+    behind = {2: send_edges, 3: lambda: send_sides(0), JOBS - 1: lambda: send_sides(1)}
+
+    wait_sides(0, 0)
     transport(0, da)
 
-    def pair(i, carry):
-        for k, (here, there) in enumerate(((da, db), (db, da))):
-            job = 2 * i + k
-            before(job)
-            transport(jnp.minimum(job + 1, 2 * JOBS - 1), there)
-            chemistry(job, here)
-            after(job)
+    for step in range(2):
+
+        def pair(i, carry):
+            for k, (here, there) in enumerate(((da, db), (db, da))):
+                job = 2 * i + k
+                for at, act in ahead.items():
+                    if at // JOBS == step and at % 2 == k:
+                        pl.when(job == at)(act)
+                transport(jnp.minimum(job + 1, 2 * JOBS - 1), there)
+                chemistry(step, job, here)
+                for at, act in behind.items():
+                    if at // JOBS == step and at % 2 == k:
+                        pl.when(job == at)(act)
+            return carry
+
+        lax.fori_loop(step * JOBS // 2, (step + 1) * JOBS // 2, pair, 0)
+
+    def last_level(l, carry):
+        for half in range(ROWS // 8):
+            for s in range(0, S, 8):
+                rows = X[2, 1 + 8 * half : 9 + 8 * half, l, s : s + 8, :]
+                out[s : s + 8, l, 8 * half : 8 * half + 8, :] = jnp.swapaxes(rows, 0, 1)
         return carry
 
-    lax.fori_loop(0, JOBS, pair, 0)
-    pltpu.make_async_copy(X.at[0, 1 : ROWS + 1], X.at[2, 1 : ROWS + 1], out_sem).wait()
+    lax.fori_loop(0, LEV, last_level, 0)
 
 
 def on_device(latent_field, east_courant, north_courant, mixing, sunlit, decode_w, react_a, react_b, stoich, encode_w, rate_const):
     coefficient = pltpu.VMEM((LEV, ROWS, COLS), F32)
-    tile = pltpu.VMEM((2, LEV, S, COLS), F32)
+    tile = pltpu.VMEM((2, LEV, 2 * S, COLS), F32)
     n_species, n_reactions = stoich.shape
     return pl.pallas_call(
         kernel,
         name="split_steps",
-        out_shape=jax.ShapeDtypeStruct(latent_field.shape, F32),
+        out_shape=pltpu.VMEM(latent_field.shape, F32),
         in_specs=[pl.BlockSpec(memory_space=pl.ANY)] * 11,
-        out_specs=pl.BlockSpec(memory_space=pl.ANY),
+        out_specs=pl.BlockSpec(memory_space=pltpu.VMEM),
         scratch_shapes=[
+            pltpu.VMEM((S, LEV, ROWS, COLS), F32),
             pltpu.VMEM((3, ROWS + 2, LEV, S, COLS), F32), tile, tile,
+            pltpu.VMEM((LEV, 2, COLS), F32),
             coefficient, coefficient, coefficient, coefficient, coefficient, coefficient,
             coefficient, coefficient, coefficient,
             coefficient, coefficient, pltpu.VMEM((LEV - 1, ROWS, COLS), F32),
@@ -329,13 +361,12 @@
             pltpu.VMEM((n_species, n_reactions), BF16), pltpu.VMEM((n_species, n_reactions), BF16),
             pltpu.VMEM((n_species, n_reactions), BF16), pltpu.VMEM((S, n_species), BF16),
             pltpu.VMEM((1, n_reactions), F32),
-            pltpu.VMEM((n_reactions, S), BF16), pltpu.VMEM((n_reactions, S), BF16),
-            pltpu.VMEM((S, n_reactions), BF16),
-            pltpu.VMEM((3, 2, S, COLS), F32), pltpu.VMEM((2, 2, S, COLS), F32),
+            pltpu.VMEM((S, S * (S // 2 + 1)), BF16), tile,
+            pltpu.VMEM((2, 2, S, COLS), F32), pltpu.VMEM((2, 2, S, COLS), F32),
             pltpu.VMEM((2, 2, S, COLS), F32), pltpu.VMEM((2, 2, S, COLS), F32),
             pltpu.VMEM((2, LEV, S, COLS), F32), pltpu.VMEM((2, LEV, S, COLS), F32),
-            pltpu.SemaphoreType.DMA((ROWS,)), pltpu.SemaphoreType.DMA((4,)),
-            pltpu.SemaphoreType.DMA((6,)), pltpu.SemaphoreType.DMA,
+            pltpu.SemaphoreType.DMA((LEV,)), pltpu.SemaphoreType.DMA((4,)),
+            pltpu.SemaphoreType.DMA((6,)),
             pltpu.SemaphoreType.DMA((2, 6)), pltpu.SemaphoreType.DMA((2, 6)),
         ],
         compiler_params=pltpu.CompilerParams(

time: 48.8 us -> 34.7 us (0.71)
  Pallas kernels: 45.4 us -> 33.2 us
  local copies, waits for them, and re-layouts: 3.13 us -> 1.32 us
    pallas_call x1, Pallas kernels: 45.4 us -> 33.2 us  [on_device(): pl.pallas_call(kernel, name='split_steps', out_shape=pltpu.VMEM(latent_fi...]
    unnamed x1, local copies, waits for them, and re-layouts: 3.13 us -> 1.32 us
where the time goes in v3:
time: 34.7 us; the launch traced here: 34.5 us
  Pallas kernels  33.2 us (96%)
  local copies, waits for them, and re-layouts  1.32 us (4%)
    pallas_call x1, Pallas kernels, on_device(): pl.pallas_call(kernel, name='split_steps', out_shape=pltpu.VMEM(latent_fi...  33.2 us
    unnamed x1, local copies, waits for them, and re-layouts  1.32 us

profile of v3, /device:TPU:6, one launch (start us, length us, event | category | flops | bytes accessed | tf_op | source)
XLA Modules:
  0.0 34.5 jit_solution(11056903516790122290)
XLA Ops:
  0.0 33.2 %split_steps.1 = f32[32,8,16,128]{3,2,1,0:T(8,128)S(1)} custom-call(f32[32,8,16,128]{3,2,1,0:T(8,128)} %x_hbm.1, f32[8,16,128]{2,1,0:T(8,128)} %ce_hbm.1, f32[8,16,128]{2,1,0:T(8,128)} %cn_hbm.1, f32[7,16,128]{2,1,0:T(8,128)} %mix_hbm.1, s32[1,8]{1,0:T(1,128)} %sun_hbm.1, bf16[32,224]{1,0:T(8,128)(2,1)} %bitcast.6, bf16[224,256]{1,0:T(8,128)(2,1)} %bitcast.4, ...), custom_call_target="tpu_custom_call" | custom-call | tf_op jit(solution)/shard_map/split_steps/pallas_call | solution.py:346
  33.2 1.3 %copy.13 = f32[32,8,16,128]{3,2,1,0:T(8,128)} copy(f32[32,8,16,128]{3,2,1,0:T(8,128)S(1)} %split_steps.1) | data formatting | bytes 4194304

commit v4 on v3

v4 whole, which is shorter than its diff:
```python
import jax
import jax.numpy as jnp
from jax import lax
from jax.experimental import pallas as pl
from jax.experimental.pallas import tpu as pltpu
from jax.sharding import PartitionSpec as P

S = 32
LEV = 8
ROWS = 16
COLS = 128
BLOCK = 16
JOBS = ROWS // 2
F32 = jnp.float32
BF16 = jnp.bfloat16
MESH = pl.DeviceIdType.MESH


def dot(a, b):
    return jnp.dot(a, b, preferred_element_type=F32)


def dot_t(a, b):
    return lax.dot_general(a, b, (((1,), (1,)), ((), ())), preferred_element_type=F32)


def kernel(
    x_hbm, ce_hbm, cn_hbm, mix_hbm, sun_hbm, dec_hbm, ra_hbm, rb_hbm, st_hbm, en_hbm, rc_hbm,
    out,
    raw, X, da, db, edge, w0, epw, emw, epm, nps, nms, lower, upper, inv,
    side_lower, side_upper, side_inv, side_epm,
    ce, cn, mix, sun, mask, dec, ra, rb, st, en, rc, quad, mid,
    packed, west, east, columns, sides, sides_mid, sides_out, to_north, to_south,
    level_sem, small_sem, weight_sem, send_sem, recv_sem,
):
    n_lat, n_lon = lax.axis_size("lat"), lax.axis_size("lon")
    lat, lon = lax.axis_index("lat"), lax.axis_index("lon")
    north, south = {"lat": lax.rem(lat + 1, n_lat)}, {"lat": lax.rem(lat + n_lat - 1, n_lat)}
    right, left = {"lon": lax.rem(lon + 1, n_lon)}, {"lon": lax.rem(lon + n_lon - 1, n_lon)}

    barrier = pltpu.get_barrier_semaphore()
    for neighbour in (north, south, right, left):
        pl.semaphore_signal(barrier, inc=1, device_id=neighbour, device_id_type=MESH)

    small = [
        pltpu.make_async_copy(a, b, small_sem.at[i])
        for i, (a, b) in enumerate(((ce_hbm, ce), (cn_hbm, cn), (mix_hbm, mix), (sun_hbm, sun)))
    ]
    weights = [
        pltpu.make_async_copy(a, b, weight_sem.at[i])
        for i, (a, b) in enumerate(
            ((dec_hbm, dec), (ra_hbm, ra), (rb_hbm, rb), (st_hbm, st), (en_hbm, en), (rc_hbm, rc))
        )
    ]
    for copy in small:
        copy.start()

    def level_copy(l):
        return pltpu.make_async_copy(x_hbm.at[:, l], raw.at[:, l], level_sem.at[l])

    for l in range(LEV):
        level_copy(l).start()
    for copy in weights:
        copy.start()

    for copy in small:
        copy.wait()
    lane = lax.broadcasted_iota(jnp.int32, (ROWS, COLS), 1)
    row = lax.broadcasted_iota(jnp.int32, (ROWS, COLS), 0)
    grid_row = row + lat * ROWS
    open_north, open_south = grid_row < n_lat * ROWS - 1, grid_row > 0
    for l in range(LEV):
        c, n = ce[l], cn[l]
        e_plus, e_minus = jnp.maximum(c, 0.0), jnp.minimum(c, 0.0)
        n_plus = jnp.where(open_north, jnp.maximum(n, 0.0), 0.0)
        n_minus = jnp.where(open_south, jnp.minimum(n, 0.0), 0.0)
        epw[l] = jnp.where(lane == 0, 0.0, pltpu.roll(e_plus, 1, 1))
        emw[l] = jnp.where(lane == COLS - 1, 0.0, pltpu.roll(e_minus, COLS - 1, 1))
        epm[l] = jnp.where(lane == COLS - 1, e_plus, e_minus)
        w0[l] = 1.0 - (e_plus - e_minus) - (n_plus - n_minus)
        nps[l] = jnp.where(row == 0, 1.0, pltpu.roll(n_plus, 1, 0))
        nms[l] = jnp.where(row == ROWS - 1, 1.0, pltpu.roll(n_minus, ROWS - 1, 0))
        edge[l, 0:1], edge[l, 1:2] = n_plus[ROWS - 1 :], n_minus[0:1]

    def edge_copies(step):
        return (
            pltpu.make_async_remote_copy(
                src_ref=to_north.at[step], dst_ref=X.at[step, 0],
                send_sem=send_sem.at[step, 0], recv_sem=recv_sem.at[step, 0],
                device_id=north, device_id_type=MESH,
            ),
            pltpu.make_async_remote_copy(
                src_ref=to_south.at[step], dst_ref=X.at[step, ROWS + 1],
                send_sem=send_sem.at[step, 1], recv_sem=recv_sem.at[step, 1],
                device_id=south, device_id_type=MESH,
            ),
        )

    def side_copies(step):
        return (
            pltpu.make_async_remote_copy(
                src_ref=packed.at[step], dst_ref=west.at[step],
                send_sem=send_sem.at[step, 2], recv_sem=recv_sem.at[step, 2],
                device_id=right, device_id_type=MESH,
            ),
            pltpu.make_async_remote_copy(
                src_ref=packed.at[step], dst_ref=east.at[step],
                send_sem=send_sem.at[step, 3], recv_sem=recv_sem.at[step, 3],
                device_id=left, device_id_type=MESH,
            ),
        )

    wide_lane = lax.broadcasted_iota(jnp.int32, (S, COLS), 1)
    packed[...] = jnp.zeros_like(packed)
    columns[...] = jnp.zeros_like(columns)

    def first_level(l, carry):
        level_copy(l).wait()
        group, start = l // 4, 32 * lax.rem(l, 4)
        line = packed[0, group]
        pair = wide_lane // 2 - start // 2
        for half in range(ROWS // 8):
            parts = [
                jnp.swapaxes(raw[s : s + 8, l, 8 * half : 8 * half + 8, :], 0, 1)
                for s in range(0, S, 8)
            ]
            for k in range(8):
                r = 8 * half + k
                value = jnp.concatenate([part[k] for part in parts], axis=0)
                X[0, r + 1, l] = value
                if r == 0:
                    to_south[0, l] = value * edge[l, 1:2]
                if r == ROWS - 1:
                    to_north[0, l] = value * edge[l, 0:1]
                moved = pltpu.roll(value * epm[l, r : r + 1, :], start + 2 * r + 1, 1)
                line = jnp.where(pair == r, moved, line)
        packed[0, group] = line
        return carry

    lax.fori_loop(0, LEV, first_level, 0)
    def send_first():
        pl.semaphore_wait(barrier, 4)
        for copy in side_copies(0) + edge_copies(0):
            copy.start()

    pl.when(lon > 0)(send_first)

    pivot_upper = None
    for l in range(LEV):
        below = mix[l - 1] if l > 0 else None
        above = mix[l] if l < LEV - 1 else None
        pivot = 1.0
        if below is not None:
            pivot = pivot + below
        if above is not None:
            pivot = pivot + above
        if below is not None:
            pivot = pivot - below * pivot_upper
            lower[l] = below
        recip = 1.0 / pivot
        inv[l] = recip
        if above is not None:
            pivot_upper = above * recip
            upper[l] = pivot_upper
    def side_form(rows):
        rows = pltpu.roll(rows, 1, 1, stride=2, stride_axis=0)
        return jnp.sum(jnp.where(lane // 2 == row, rows, 0.0), axis=0, keepdims=True)

    side_epm[...] = jnp.zeros_like(side_epm)
    for l in range(LEV):
        side_inv[l] = side_form(inv[l])
        if l > 0:
            side_lower[l] = side_form(lower[l])
        if l < LEV - 1:
            side_upper[l] = side_form(upper[l])
        side_epm[l // 4] = side_epm[l // 4] + pltpu.roll(side_form(epm[l]), 32 * (l % 4), 1)
    block = lax.broadcasted_iota(jnp.int32, (1, COLS), 1) // BLOCK
    lit = jnp.zeros((1, COLS), jnp.int32)
    for b in range(COLS // BLOCK):
        lit = jnp.where(block == b, sun[0:1, b : b + 1], lit)
    mask[...] = lit
    for copy in weights:
        copy.wait()
    a = dot(dec[...], ra[...])
    b = dot(dec[...], rb[...])
    e = dot(en[...], st[...]) * rc[...]
    pairs = []
    for d in range(S // 2 + 1):
        a_on = a if d == 0 else jnp.concatenate([a[d:], a[:d]], axis=0)
        b_on = b if d == 0 else jnp.concatenate([b[d:], b[:d]], axis=0)
        pairs.append(a * b_on if d in (0, S // 2) else a * b_on + a_on * b)
    pairs = jnp.concatenate(pairs, axis=0)
    pairs_top, e_top = pairs.astype(BF16), e.astype(BF16)
    pairs_rest = (pairs - pairs_top.astype(F32)).astype(BF16)
    e_rest = (e - e_top.astype(F32)).astype(BF16)
    quad[...] = (
        dot_t(e_top, pairs_top) + (dot_t(e_rest, pairs_top) + dot_t(e_top, pairs_rest))
    ).astype(BF16)

    def rows_of(job):
        return lax.rem(2 * job + 1, ROWS), lax.rem(2 * job + 2, ROWS)

    def transport(step, job, dest):
        lines = [columns[0], columns[1]]
        for k, r in enumerate(rows_of(job)):
            solved = []
            for l in range(LEV):
                at = lambda ref: ref[l, pl.ds(r, 1), :]
                q = X[step, r + 1, l]
                value = (
                    q * at(w0)
                    + (pltpu.roll(q, 1, 1) * at(epw) - pltpu.roll(q, COLS - 1, 1) * at(emw))
                    + (X[step, r, l] * at(nps) - X[step, r + 2, l] * at(nms))
                )
                if l > 0:
                    value = value + at(lower) * solved[-1]
                solved.append(value * at(inv))
            value = solved[-1]
            pair = wide_lane // 2 - r
            for l in range(LEV - 1, -1, -1):
                if l < LEV - 1:
                    value = solved[l] + upper[l, pl.ds(r, 1), :] * value
                dest[k, l, 0:S] = value
                dest[k, l, S:] = value
                start = 32 * (l % 4)
                moved = pltpu.roll(value, start + 2 * r + 1, 1)
                lines[l // 4] = jnp.where(pair == start // 2, moved, lines[l // 4])
        columns[0], columns[1] = lines

    def products(ref):
        shifted = [ref[0 : 3 * S // 2]]
        shifted += [ref[b : b + S + 8] for b in range(1, 8)]
        lines = shifted[0][0:S].astype(BF16)
        return jnp.concatenate(
            [
                lines * shifted[d % 8][d // 8 * 8 : d // 8 * 8 + S].astype(BF16)
                for d in range(S // 2 + 1)
            ],
            axis=0,
        )

    def changes(first, second):
        change = dot(quad[...], jnp.concatenate([products(first), products(second)], axis=1))
        return change[:, :COLS], change[:, COLS:]

    lit_lanes = jnp.broadcast_to(mask[...], (S, COLS)) > 0
    lit_sides = (
        jnp.broadcast_to(
            jnp.where(
                lax.rem(lax.broadcasted_iota(jnp.int32, (1, COLS), 1), 2) == 0,
                sun[0:1, COLS // BLOCK - 1 :],
                sun[0:1, 0:1],
            ),
            (S, COLS),
        )
        > 0
    )

    def chemistry(step, job, source):
        for k in range(2):
            for l in range(0, LEV, 2):
                for h, change in enumerate(changes(source.at[k, l], source.at[k, l + 1])):
                    value = source[k, l + h, 0:S] + change
                    mid[k, l + h, 0:S] = value
                    mid[k, l + h, S:] = value
        for k, r in enumerate(rows_of(job)):
            for l in range(0, LEV, 2):
                for h, change in enumerate(changes(mid.at[k, l], mid.at[k, l + 1])):
                    X[step + 1, r + 1, l + h] = jnp.where(
                        lit_lanes, mid[k, l + h, 0:S] + change, source[k, l + h, 0:S]
                    )

    def edge_columns(step):
        even = lax.rem(wide_lane, 2) == 0
        arrived = [
            jnp.where(
                even,
                -pltpu.roll(east[step, group], COLS - 1, 1),
                pltpu.roll(west[step, group], 1, 1),
            )
            for group in range(2)
        ]
        solved = []
        for l in range(LEV):
            value = pltpu.roll(arrived[l // 4], (COLS - 32 * (l % 4)) % COLS, 1)
            if l > 0:
                value = value + side_lower[l] * solved[-1]
            solved.append(value * side_inv[l])
        total = [columns[0], columns[1]]
        value = solved[-1]
        for l in range(LEV - 1, -1, -1):
            if l < LEV - 1:
                value = solved[l] + side_upper[l] * value
            total[l // 4] = total[l // 4] + pltpu.roll(value, 32 * (l % 4), 1)
        for group in range(2):
            sides[group, 0:S] = total[group]
            sides[group, S:] = total[group]
        for group, change in enumerate(changes(sides.at[0], sides.at[1])):
            value = total[group] + change
            sides_mid[group, 0:S] = value
            sides_mid[group, S:] = value
        for group, change in enumerate(changes(sides_mid.at[0], sides_mid.at[1])):
            value = jnp.where(lit_sides, sides_mid[group, 0:S] + change, total[group])
            sides_out[group] = value
            if step == 0:
                packed[1, group] = value * side_epm[group]

    edge_lane = lax.rem(lax.broadcasted_iota(jnp.int32, (8, COLS), 1) + 1, COLS) < 2

    def patched(line, values, l, r):
        shift = COLS - (32 * lax.rem(l, 4) + 2 * r + 1)
        return jnp.where(edge_lane, pltpu.roll(line, shift, 1), values)

    def patch_level(l, carry):
        for s in range(0, S, 8):
            line = sides_out[l // 4, s : s + 8]
            for r in range(ROWS):
                X[1, r + 1, l, s : s + 8] = patched(line, X[1, r + 1, l, s : s + 8], l, r)
        return carry

    def send_edges():
        for l in range(LEV):
            to_north[1, l] = X[1, ROWS, l] * edge[l, 0:1]
            to_south[1, l] = X[1, 1, l] * edge[l, 1:2]
        for copy in edge_copies(1):
            copy.start()

    for step in range(2):
        transport(step, 0, da)

        def pair(i, carry):
            transport(step, 2 * i + 1, db)
            chemistry(step, 2 * i, da)
            transport(step, 2 * i + 2, da)
            chemistry(step, 2 * i + 1, db)
            if step == 0:
                pl.when((i == 1) & (lon == 0))(send_first)
            return carry

        lax.fori_loop(0, JOBS // 2 - 1, pair, 0)
        for copy in edge_copies(step):
            copy.wait()
        transport(step, JOBS - 1, db)
        chemistry(step, JOBS - 2, da)
        for copy in side_copies(step):
            copy.wait()
        edge_columns(step)
        chemistry(step, JOBS - 1, db)
        if step == 0:
            for copy in side_copies(1):
                copy.start()
            lax.fori_loop(0, LEV, patch_level, 0)
            send_edges()

    def last_level(l, carry):
        for s in range(0, S, 8):
            line = sides_out[l // 4, s : s + 8]
            for half in range(ROWS // 8):
                rows = [
                    patched(line, X[2, 8 * half + k + 1, l, s : s + 8], l, 8 * half + k)
                    for k in range(8)
                ]
                out[s : s + 8, l, 8 * half : 8 * half + 8, :] = jnp.swapaxes(jnp.stack(rows), 0, 1)
        return carry

    lax.fori_loop(0, LEV, last_level, 0)


def on_device(latent_field, east_courant, north_courant, mixing, sunlit, decode_w, react_a, react_b, stoich, encode_w, rate_const):
    coefficient = pltpu.VMEM((LEV, ROWS, COLS), F32)
    tile = pltpu.VMEM((2, LEV, 2 * S, COLS), F32)
    side = pltpu.VMEM((LEV, 1, COLS), F32)
    n_species, n_reactions = stoich.shape
    return pl.pallas_call(
        kernel,
        name="split_steps",
        out_shape=pltpu.VMEM(latent_field.shape, F32),
        in_specs=[pl.BlockSpec(memory_space=pl.ANY)] * 11,
        out_specs=pl.BlockSpec(memory_space=pltpu.VMEM),
        scratch_shapes=[
            pltpu.VMEM((S, LEV, ROWS, COLS), F32),
            pltpu.VMEM((3, ROWS + 2, LEV, S, COLS), F32), tile, tile,
            pltpu.VMEM((LEV, 2, COLS), F32),
            coefficient, coefficient, coefficient, coefficient, coefficient, coefficient,
            coefficient, coefficient, coefficient,
            side, side, side, pltpu.VMEM((2, 1, COLS), F32),
            coefficient, coefficient, pltpu.VMEM((LEV - 1, ROWS, COLS), F32),
            pltpu.VMEM((1, COLS // BLOCK), jnp.int32), pltpu.VMEM((1, COLS), jnp.int32),
            pltpu.VMEM((S, n_species), BF16),
            pltpu.VMEM((n_species, n_reactions), BF16), pltpu.VMEM((n_species, n_reactions), BF16),
            pltpu.VMEM((n_species, n_reactions), BF16), pltpu.VMEM((S, n_species), BF16),
            pltpu.VMEM((1, n_reactions), F32),
            pltpu.VMEM((S, S * (S // 2 + 1)), BF16), tile,
            pltpu.VMEM((2, 2, S, COLS), F32), pltpu.VMEM((2, 2, S, COLS), F32),
            pltpu.VMEM((2, 2, S, COLS), F32), pltpu.VMEM((2, S, COLS), F32),
            pltpu.VMEM((2, 2 * S, COLS), F32), pltpu.VMEM((2, 2 * S, COLS), F32),
            pltpu.VMEM((2, S, COLS), F32),
            pltpu.VMEM((2, LEV, S, COLS), F32), pltpu.VMEM((2, LEV, S, COLS), F32),
            pltpu.SemaphoreType.DMA((LEV,)), pltpu.SemaphoreType.DMA((4,)),
            pltpu.SemaphoreType.DMA((6,)),
            pltpu.SemaphoreType.DMA((2, 4)), pltpu.SemaphoreType.DMA((2, 4)),
        ],
        compiler_params=pltpu.CompilerParams(
            collective_id=0, has_side_effects=True
        ),
    )(
        latent_field, east_courant, north_courant, mixing, sunlit, decode_w.T, react_a.T,
        react_b.T, stoich, encode_w, rate_const.reshape(1, -1),
    )


def solution(mesh):
    placed = (
        P(None, None, "lat", "lon"),
        P(None, "lat", "lon"),
        P(None, "lat", "lon"),
        P(None, "lat", "lon"),
        P("lat", "lon"),
        P(),
        P(),
        P(),
        P(),
        P(),
        P(),
    )
    return jax.shard_map(
        on_device,
        mesh=mesh,
        in_specs=placed,
        out_specs=P(None, None, "lat", "lon"),
        check_vma=False,
    )
```

time: 34.7 us -> 28.6 us (0.82)
  the two profiles are of different devices: /device:TPU:6 before, /device:TPU:1 now
where the time goes in v4:
time: 28.6 us; the launch traced here: 28.5 us
  Pallas kernels  27.2 us (95%)
  local copies, waits for them, and re-layouts  1.32 us (5%)
    pallas_call x1, Pallas kernels, on_device(): pl.pallas_call(kernel, name='split_steps', out_shape=pltpu.VMEM(latent_fi...  27.2 us
    unnamed x1, local copies, waits for them, and re-layouts  1.32 us

profile of v4, /device:TPU:1, one launch (start us, length us, event | category | flops | bytes accessed | tf_op | source)
XLA Modules:
  0.0 28.5 jit_solution(10573032353256302426)
XLA Ops:
  0.0 27.2 %split_steps.1 = f32[32,8,16,128]{3,2,1,0:T(8,128)S(1)} custom-call(f32[32,8,16,128]{3,2,1,0:T(8,128)} %x_hbm.1, f32[8,16,128]{2,1,0:T(8,128)} %ce_hbm.1, f32[8,16,128]{2,1,0:T(8,128)} %cn_hbm.1, f32[7,16,128]{2,1,0:T(8,128)} %mix_hbm.1, s32[1,8]{1,0:T(1,128)} %sun_hbm.1, bf16[32,224]{1,0:T(8,128)(2,1)} %bitcast.6, bf16[224,256]{1,0:T(8,128)(2,1)} %bitcast.4, ...), custom_call_target="tpu_custom_call" | custom-call | tf_op jit(solution)/shard_map/split_steps/pallas_call | solution.py:374
  27.2 1.3 %copy.13 = f32[32,8,16,128]{3,2,1,0:T(8,128)} copy(f32[32,8,16,128]{3,2,1,0:T(8,128)S(1)} %split_steps.1) | data formatting | bytes 4194304

commit v5 on v4

--- a/solution.py
+++ b/solution.py
@@ -24,13 +24,18 @@
     return lax.dot_general(a, b, (((1,), (1,)), ((), ())), preferred_element_type=F32)
 
 
+def patched(line, values, edge_lane, l, r):
+    shift = COLS - (32 * (l % 4) + 2 * r + 1)
+    return jnp.where(edge_lane, pltpu.roll(line, shift, 1), values)
+
+
 def kernel(
     x_hbm, ce_hbm, cn_hbm, mix_hbm, sun_hbm, dec_hbm, ra_hbm, rb_hbm, st_hbm, en_hbm, rc_hbm,
-    out,
+    rows_out, sides_out,
     raw, X, da, db, edge, w0, epw, emw, epm, nps, nms, lower, upper, inv,
     side_lower, side_upper, side_inv, side_epm,
     ce, cn, mix, sun, mask, dec, ra, rb, st, en, rc, quad, mid,
-    packed, west, east, columns, sides, sides_mid, sides_out, to_north, to_south,
+    packed, west, east, columns, sides, sides_mid, to_north, to_south,
     level_sem, small_sem, weight_sem, send_sem, recv_sem,
 ):
     n_lat, n_lon = lax.axis_size("lat"), lax.axis_size("lon")
@@ -114,6 +119,35 @@
     packed[...] = jnp.zeros_like(packed)
     columns[...] = jnp.zeros_like(columns)
 
+    pivot_upper = None
+    for l in range(LEV):
+        below = mix[l - 1] if l > 0 else None
+        above = mix[l] if l < LEV - 1 else None
+        pivot = 1.0
+        if below is not None:
+            pivot = pivot + below
+        if above is not None:
+            pivot = pivot + above
+        if below is not None:
+            pivot = pivot - below * pivot_upper
+            lower[l] = below
+        recip = 1.0 / pivot
+        inv[l] = recip
+        if above is not None:
+            pivot_upper = above * recip
+            upper[l] = pivot_upper
+    def side_form(rows):
+        rows = pltpu.roll(rows, 1, 1, stride=2, stride_axis=0)
+        return jnp.sum(jnp.where(lane // 2 == row, rows, 0.0), axis=0, keepdims=True)
+
+    side_epm[...] = jnp.zeros_like(side_epm)
+    for l in range(LEV):
+        side_inv[l] = side_form(inv[l])
+        if l > 0:
+            side_lower[l] = side_form(lower[l])
+        if l < LEV - 1:
+            side_upper[l] = side_form(upper[l])
+        side_epm[l // 4] = side_epm[l // 4] + pltpu.roll(side_form(epm[l]), 32 * (l % 4), 1)
     def first_level(l, carry):
         level_copy(l).wait()
         group, start = l // 4, 32 * lax.rem(l, 4)
@@ -145,35 +179,6 @@
 
     pl.when(lon > 0)(send_first)
 
-    pivot_upper = None
-    for l in range(LEV):
-        below = mix[l - 1] if l > 0 else None
-        above = mix[l] if l < LEV - 1 else None
-        pivot = 1.0
-        if below is not None:
-            pivot = pivot + below
-        if above is not None:
-            pivot = pivot + above
-        if below is not None:
-            pivot = pivot - below * pivot_upper
-            lower[l] = below
-        recip = 1.0 / pivot
-        inv[l] = recip
-        if above is not None:
-            pivot_upper = above * recip
-            upper[l] = pivot_upper
-    def side_form(rows):
-        rows = pltpu.roll(rows, 1, 1, stride=2, stride_axis=0)
-        return jnp.sum(jnp.where(lane // 2 == row, rows, 0.0), axis=0, keepdims=True)
-
-    side_epm[...] = jnp.zeros_like(side_epm)
-    for l in range(LEV):
-        side_inv[l] = side_form(inv[l])
-        if l > 0:
-            side_lower[l] = side_form(lower[l])
-        if l < LEV - 1:
-            side_upper[l] = side_form(upper[l])
-        side_epm[l // 4] = side_epm[l // 4] + pltpu.roll(side_form(epm[l]), 32 * (l % 4), 1)
     block = lax.broadcasted_iota(jnp.int32, (1, COLS), 1) // BLOCK
     lit = jnp.zeros((1, COLS), jnp.int32)
     for b in range(COLS // BLOCK):
@@ -266,9 +271,13 @@
         for k, r in enumerate(rows_of(job)):
             for l in range(0, LEV, 2):
                 for h, change in enumerate(changes(mid.at[k, l], mid.at[k, l + 1])):
-                    X[step + 1, r + 1, l + h] = jnp.where(
+                    value = jnp.where(
                         lit_lanes, mid[k, l + h, 0:S] + change, source[k, l + h, 0:S]
                     )
+                    if step == 0:
+                        X[1, r + 1, l + h] = value
+                    else:
+                        rows_out[r, l + h] = value
 
     def edge_columns(step):
         even = lax.rem(wide_lane, 2) == 0
@@ -307,15 +316,13 @@
 
     edge_lane = lax.rem(lax.broadcasted_iota(jnp.int32, (8, COLS), 1) + 1, COLS) < 2
 
-    def patched(line, values, l, r):
-        shift = COLS - (32 * lax.rem(l, 4) + 2 * r + 1)
-        return jnp.where(edge_lane, pltpu.roll(line, shift, 1), values)
-
     def patch_level(l, carry):
         for s in range(0, S, 8):
             line = sides_out[l // 4, s : s + 8]
             for r in range(ROWS):
-                X[1, r + 1, l, s : s + 8] = patched(line, X[1, r + 1, l, s : s + 8], l, r)
+                X[1, r + 1, l, s : s + 8] = patched(
+                    line, X[1, r + 1, l, s : s + 8], edge_lane, l, r
+                )
         return carry
 
     def send_edges():
@@ -334,7 +341,7 @@
             transport(step, 2 * i + 2, da)
             chemistry(step, 2 * i + 1, db)
             if step == 0:
-                pl.when((i == 1) & (lon == 0))(send_first)
+                pl.when((i == 0) & (lon == 0))(send_first)
             return carry
 
         lax.fori_loop(0, JOBS // 2 - 1, pair, 0)
@@ -352,18 +359,27 @@
             lax.fori_loop(0, LEV, patch_level, 0)
             send_edges()
 
-    def last_level(l, carry):
+
+def finish(rows_in, sides_out, out, whole, sem):
+    edge_lane = lax.rem(lax.broadcasted_iota(jnp.int32, (8, COLS), 1) + 1, COLS) < 2
+
+    def level_copy(l):
+        return pltpu.make_async_copy(whole.at[:, l], out.at[:, l], sem.at[l])
+
+    for l in range(LEV):
         for s in range(0, S, 8):
             line = sides_out[l // 4, s : s + 8]
             for half in range(ROWS // 8):
                 rows = [
-                    patched(line, X[2, 8 * half + k + 1, l, s : s + 8], l, 8 * half + k)
-                    for k in range(8)
+                    patched(line, rows_in[r, l, s : s + 8], edge_lane, l, r)
+                    for r in range(8 * half, 8 * half + 8)
                 ]
-                out[s : s + 8, l, 8 * half : 8 * half + 8, :] = jnp.swapaxes(jnp.stack(rows), 0, 1)
-        return carry
-
-    lax.fori_loop(0, LEV, last_level, 0)
+                whole[s : s + 8, l, 8 * half : 8 * half + 8, :] = jnp.swapaxes(
+                    jnp.stack(rows), 0, 1
+                )
+        level_copy(l).start()
+    for l in range(LEV):
+        level_copy(l).wait()
 
 
 def on_device(latent_field, east_courant, north_courant, mixing, sunlit, decode_w, react_a, react_b, stoich, encode_w, rate_const):
@@ -371,15 +387,15 @@
     tile = pltpu.VMEM((2, LEV, 2 * S, COLS), F32)
     side = pltpu.VMEM((LEV, 1, COLS), F32)
     n_species, n_reactions = stoich.shape
-    return pl.pallas_call(
+    rows, sides = pl.pallas_call(
         kernel,
         name="split_steps",
-        out_shape=pltpu.VMEM(latent_field.shape, F32),
+        out_shape=(pltpu.VMEM((ROWS, LEV, S, COLS), F32), pltpu.VMEM((2, S, COLS), F32)),
         in_specs=[pl.BlockSpec(memory_space=pl.ANY)] * 11,
-        out_specs=pl.BlockSpec(memory_space=pltpu.VMEM),
+        out_specs=[pl.BlockSpec(memory_space=pltpu.VMEM)] * 2,
         scratch_shapes=[
             pltpu.VMEM((S, LEV, ROWS, COLS), F32),
-            pltpu.VMEM((3, ROWS + 2, LEV, S, COLS), F32), tile, tile,
+            pltpu.VMEM((2, ROWS + 2, LEV, S, COLS), F32), tile, tile,
             pltpu.VMEM((LEV, 2, COLS), F32),
             coefficient, coefficient, coefficient, coefficient, coefficient, coefficient,
             coefficient, coefficient, coefficient,
@@ -394,7 +410,6 @@
             pltpu.VMEM((2, 2, S, COLS), F32), pltpu.VMEM((2, 2, S, COLS), F32),
             pltpu.VMEM((2, 2, S, COLS), F32), pltpu.VMEM((2, S, COLS), F32),
             pltpu.VMEM((2, 2 * S, COLS), F32), pltpu.VMEM((2, 2 * S, COLS), F32),
-            pltpu.VMEM((2, S, COLS), F32),
             pltpu.VMEM((2, LEV, S, COLS), F32), pltpu.VMEM((2, LEV, S, COLS), F32),
             pltpu.SemaphoreType.DMA((LEV,)), pltpu.SemaphoreType.DMA((4,)),
             pltpu.SemaphoreType.DMA((6,)),
@@ -407,6 +422,15 @@
         latent_field, east_courant, north_courant, mixing, sunlit, decode_w.T, react_a.T,
         react_b.T, stoich, encode_w, rate_const.reshape(1, -1),
     )
+    return pl.pallas_call(
+        finish,
+        name="finish",
+        out_shape=jax.ShapeDtypeStruct(latent_field.shape, F32),
+        in_specs=[pl.BlockSpec(memory_space=pltpu.VMEM)] * 2,
+        out_specs=pl.BlockSpec(memory_space=pl.ANY),
+        scratch_shapes=[pltpu.VMEM((S, LEV, ROWS, COLS), F32), pltpu.SemaphoreType.DMA((LEV,))],
+        compiler_params=pltpu.CompilerParams(vmem_limit_bytes=24 << 20),
+    )(rows, sides)
 
 
 def solution(mesh):

time: 28.6 us -> 26.1 us (0.913)
  local copies, waits for them, and re-layouts: 1.32 us -> 0 us
  Pallas kernels: 27.2 us -> 25.9 us
    unnamed x1 -> x0, local copies, waits for them, and re-layouts: 1.32 us -> none
    pallas_call x1 -> x2, Pallas kernels: 27.2 us -> 25.9 us  [the longest x1 24.4 us: on_device(): pl.pallas_call(kernel, name='split_steps', out_shape=(pltpu.VMEM((ROWS, L...]
where the time goes in v5:
time: 26.1 us; the launch traced here: 25.9 us
  Pallas kernels  25.9 us (99%)
    pallas_call x1, Pallas kernels, on_device(): pl.pallas_call(kernel, name='split_steps', out_shape=(pltpu.VMEM((ROWS, L...  24.4 us
    pallas_call x1, Pallas kernels, on_device(): pl.pallas_call(finish, name='finish', out_shape=jax.ShapeDtypeStruct(late...  1.52 us

profile of v5, /device:TPU:1, one launch (start us, length us, event | category | flops | bytes accessed | tf_op | source)
XLA Modules:
  0.0 25.9 jit_solution(17471163362148184612)
XLA Ops:
  0.0 24.4 %split_steps.1 = (f32[16,8,32,128]{3,2,1,0:T(8,128)S(1)}, f32[2,32,128]{2,1,0:T(8,128)S(1)}) custom-call(f32[32,8,16,128]{3,2,1,0:T(8,128)} %x_hbm.1, f32[8,16,128]{2,1,0:T(8,128)} %ce_hbm.1, f32[8,16,128]{2,1,0:T(8,128)} %cn_hbm.1, f32[7,16,128]{2,1,0:T(8,128)} %mix_hbm.1, s32[1,8]{1,0:T(1,128)} %sun_hbm.1, bf16[32,224]{1,0:T(8,128)(2,1)} %bitcast.6, ...), custom_call_target="tpu_custom_call" | custom-call | tf_op jit(solution)/shard_map/split_steps/pallas_call | solution.py:390
  24.4 1.5 %finish.1 = f32[32,8,16,128]{3,2,1,0:T(8,128)} custom-call(f32[16,8,32,128]{3,2,1,0:T(8,128)S(1)} %get-tuple-element.7.rows_in, f32[2,32,128]{2,1,0:T(8,128)S(1)} %get-tuple-element.8.sides_out), custom_call_target="tpu_custom_call" | custom-call | tf_op jit(solution)/shard_map/finish/pallas_call | solution.py:425

commit v6 on v5

--- a/solution.py
+++ b/solution.py
@@ -43,10 +43,6 @@
     north, south = {"lat": lax.rem(lat + 1, n_lat)}, {"lat": lax.rem(lat + n_lat - 1, n_lat)}
     right, left = {"lon": lax.rem(lon + 1, n_lon)}, {"lon": lax.rem(lon + n_lon - 1, n_lon)}
 
-    barrier = pltpu.get_barrier_semaphore()
-    for neighbour in (north, south, right, left):
-        pl.semaphore_signal(barrier, inc=1, device_id=neighbour, device_id_type=MESH)
-
     small = [
         pltpu.make_async_copy(a, b, small_sem.at[i])
         for i, (a, b) in enumerate(((ce_hbm, ce), (cn_hbm, cn), (mix_hbm, mix), (sun_hbm, sun)))
@@ -65,6 +61,14 @@
 
     for l in range(LEV):
         level_copy(l).start()
+    barrier = pltpu.get_barrier_semaphore()
+    enter = lambda where: pl.semaphore_signal(
+        barrier, inc=1, device_id=where, device_id_type=MESH
+    )
+    enter(north)
+    enter(south)
+    enter(left)
+
     for copy in weights:
         copy.start()
 
@@ -172,12 +176,23 @@
         return carry
 
     lax.fori_loop(0, LEV, first_level, 0)
+    def start(copies):
+        for copy in copies:
+            copy.start()
+
+    def arrive(copies):
+        for copy in copies:
+            copy.wait_recv()
+
     def send_first():
-        pl.semaphore_wait(barrier, 4)
-        for copy in side_copies(0) + edge_copies(0):
-            copy.start()
-
-    pl.when(lon > 0)(send_first)
+        pl.semaphore_wait(barrier, 3)
+        start(side_copies(0)[:1] + edge_copies(0))
+
+    def send_left_first():
+        arrive(side_copies(0)[:1])
+        start(side_copies(0)[1:])
+
+    send_first()
 
     block = lax.broadcasted_iota(jnp.int32, (1, COLS), 1) // BLOCK
     lit = jnp.zeros((1, COLS), jnp.int32)
@@ -341,7 +356,7 @@
             transport(step, 2 * i + 2, da)
             chemistry(step, 2 * i + 1, db)
             if step == 0:
-                pl.when((i == 0) & (lon == 0))(send_first)
+                pl.when((i == 1) & (lon > 0))(send_left_first)
             return carry
 
         lax.fori_loop(0, JOBS // 2 - 1, pair, 0)
@@ -349,15 +364,28 @@
             copy.wait()
         transport(step, JOBS - 1, db)
         chemistry(step, JOBS - 2, da)
-        for copy in side_copies(step):
-            copy.wait()
-        edge_columns(step)
-        chemistry(step, JOBS - 1, db)
+        early = lon == 0 if step == 0 else (lon == 0) | (lon == n_lon - 1)
+
+        @pl.when(jnp.logical_not(early))
+        def _():
+            arrive(side_copies(step)[1 - step :])
+            edge_columns(step)
+            chemistry(step, JOBS - 1, db)
+
+        @pl.when(early)
+        def _():
+            chemistry(step, JOBS - 1, db)
+            if step == 0:
+                send_left_first()
+            arrive(side_copies(step)[1 - step :])
+            edge_columns(step)
+
         if step == 0:
-            for copy in side_copies(1):
-                copy.start()
+            start(side_copies(1))
             lax.fori_loop(0, LEV, patch_level, 0)
             send_edges()
+        for copy in side_copies(step):
+            copy.wait_send()
 
 
 def finish(rows_in, sides_out, out, whole, sem):

time: 26.1 us -> 25.7 us (0.985)
  the two profiles are of different devices: /device:TPU:1 before, /device:TPU:122 now
where the time goes in v6:
time: 25.7 us; the launch traced here: 25.5 us
  Pallas kernels  25.5 us (99%)
    pallas_call x1, Pallas kernels, on_device(): pl.pallas_call(kernel, name='split_steps', out_shape=(pltpu.VMEM((ROWS, L...  24 us
    pallas_call x1, Pallas kernels, on_device(): pl.pallas_call(finish, name='finish', out_shape=jax.ShapeDtypeStruct(late...  1.52 us

profile of v6, /device:TPU:122, one launch (start us, length us, event | category | flops | bytes accessed | tf_op | source)
XLA Modules:
  0.0 25.5 jit_solution(8361793998021331820)
XLA Ops:
  0.0 24.0 %split_steps.1 = (f32[16,8,32,128]{3,2,1,0:T(8,128)S(1)}, f32[2,32,128]{2,1,0:T(8,128)S(1)}) custom-call(f32[32,8,16,128]{3,2,1,0:T(8,128)} %x_hbm.1, f32[8,16,128]{2,1,0:T(8,128)} %ce_hbm.1, f32[8,16,128]{2,1,0:T(8,128)} %cn_hbm.1, f32[7,16,128]{2,1,0:T(8,128)} %mix_hbm.1, s32[1,8]{1,0:T(1,128)} %sun_hbm.1, bf16[32,224]{1,0:T(8,128)(2,1)} %bitcast.6, ...), custom_call_target="tpu_custom_call" | custom-call | tf_op jit(solution)/shard_map/split_steps/pallas_call | solution.py:418
  24.0 1.5 %finish.1 = f32[32,8,16,128]{3,2,1,0:T(8,128)} custom-call(f32[16,8,32,128]{3,2,1,0:T(8,128)S(1)} %get-tuple-element.7.rows_in, f32[2,32,128]{2,1,0:T(8,128)S(1)} %get-tuple-element.8.sides_out), custom_call_target="tpu_custom_call" | custom-call | tf_op jit(solution)/shard_map/finish/pallas_call | solution.py:453
